TPU v7x, 128 devices: a whole 4x4x4 slice. The times are simulated.
128 devices in a mesh: sat: 16 (over x, z), dop: 8 (over y, core).
Axes of the slice: x: 4, y: 4, z: 4, core: 2. Of those that a mesh axis runs over, the one named last changes fastest.
Arguments:
- samples: float32 [2, 8192], P(None, ('sat', 'dop')), may hold values from -6 to 6
- code_chips: int32 [48, 4092], P('sat'), may hold values from -1 to 1, as said below
- centers: int32 [48], P('sat'), may hold values from -20 to 20
- widths: int32 [48], P('sat'), may hold values from 1 to 8
Outputs:
- ratio: float32 [48, 128, 8192], P('sat', None, 'dop')
Inputs may be any that keep to these rules, and one draw needn't show every extreme that they name: `code_chips`: every entry is -1 or 1.
All inputs are finite; a program needn't handle non-finite values.
Results may differ from a plain program's by a relative error of at most 0.0003.
Values sent between devices are 32-bit elements; how exact they have to be, the bound alone decides.
A program may use at most 64 MiB of HBM per device.

v0:
```python
import math

import jax
import jax.numpy as jnp
from jax import lax
from jax.sharding import Mesh
from jax.sharding import PartitionSpec as P

SAMPLES = 8192
SPLIT = 64
CHIPS = 4092
DOP = 128
SAT_DOP = ("sat", "dop_0", "dop_1")
DOP_AXES = ("dop_0", "dop_1")


highest = lax.Precision.HIGHEST


def in_blocks(shard, dim, length):
    shape = shard.shape
    parts = shard.reshape(*shape[:dim], length, shape[dim] // length, *shape[dim + 1 :])
    return jnp.moveaxis(parts, dim, 0)


def joined_along(parts, dim):
    parts = jnp.moveaxis(parts, 0, dim)
    shape = parts.shape
    return parts.reshape(*shape[:dim], shape[dim] * shape[dim + 1], *shape[dim + 2 :])


def moved_by_axis(parts, axes, turns):
    inside = parts.shape[1:]
    result = parts.reshape(*(lax.axis_size(a) for a in axes), *inside)
    for k in turns:
        result = lax.all_to_all(result, axes[k], k, k, tiled=True)
    return result.reshape(-1, *inside)


def core_and_chips(shard, groups, turns, split_dim, concat_dim):
    length = lax.axis_size(groups[0]) * lax.axis_size(groups[1])
    parts = in_blocks(shard, split_dim, length)
    return joined_along(moved_by_axis(parts, groups, turns), concat_dim)


def sent_to_all(shard, axis):
    length = lax.axis_size(axis)
    return lax.all_to_all(
        jnp.broadcast_to(shard[None], (length, *shard.shape)), axis, 0, 0, tiled=True
    )


def of_everyone(shard, axis):
    return sent_to_all(shard, axis).sum(axis=0)


def tables(length):
    index = jnp.arange(length, dtype=jnp.int32)
    turns = index[:, None] * index[None, :] % length
    angle = turns.astype(jnp.float32) * (2.0 * math.pi / length)
    return (jnp.cos(angle), jnp.sin(angle))


def twiddles(first, second):
    left = jnp.arange(first, dtype=jnp.int32)
    right = jnp.arange(second, dtype=jnp.int32)
    turns = left[:, None] * right[None, :] % (first * second)
    angle = turns.astype(jnp.float32) * (2.0 * math.pi / (first * second))
    return (jnp.cos(angle), jnp.sin(angle))


def left_mul(table, block):
    return jnp.einsum("kn,bnq->bkq", table, block, precision=highest)


def right_mul(block, table):
    return jnp.einsum("bkn,nm->bkm", block, table, precision=highest)


def forward(real, imag):
    second = real.shape[2]
    cos_p, sin_p = tables(SPLIT)
    cos_q, sin_q = tables(second)
    tw_c, tw_s = twiddles(SPLIT, second)
    part_re = left_mul(cos_p, real) + left_mul(sin_p, imag)
    part_im = left_mul(cos_p, imag) - left_mul(sin_p, real)
    turned_re = part_re * tw_c + part_im * tw_s
    turned_im = part_im * tw_c - part_re * tw_s
    out_re = right_mul(turned_re, cos_q) + right_mul(turned_im, sin_q)
    out_im = right_mul(turned_im, cos_q) - right_mul(turned_re, sin_q)
    return (out_re, out_im)


def inverse_rows(real, imag):
    second = real.shape[2]
    cos_p, sin_p = tables(SPLIT)
    cos_q, sin_q = tables(second)
    tw_c, tw_s = twiddles(SPLIT, second)
    part_re = right_mul(real, cos_q) - right_mul(imag, sin_q)
    part_im = right_mul(imag, cos_q) + right_mul(real, sin_q)
    turned_re = part_re * tw_c - part_im * tw_s
    turned_im = part_im * tw_c + part_re * tw_s
    out_re = left_mul(cos_p, turned_re) - left_mul(sin_p, turned_im)
    out_im = left_mul(cos_p, turned_im) + left_mul(sin_p, turned_re)
    return (out_re, out_im)


def signal_spectra(received, rows):
    index = jnp.arange(SAMPLES, dtype=jnp.int32)
    offsets = rows - DOP // 2
    turns = offsets[:, None] * index[None, :] % (2 * SAMPLES)
    phase = turns.astype(jnp.float32) * (2.0 * math.pi / (2 * SAMPLES))
    cosine = jnp.cos(phase)
    sine = jnp.sin(phase)
    wiped_re = received[0][None, :] * cosine + received[1][None, :] * sine
    wiped_im = received[1][None, :] * cosine - received[0][None, :] * sine
    count = rows.shape[0]
    spec_re, spec_im = forward(
        wiped_re.reshape(count, SPLIT, SAMPLES // SPLIT),
        wiped_im.reshape(count, SPLIT, SAMPLES // SPLIT),
    )
    return jnp.stack([spec_re, spec_im], axis=1)


def code_spectra(code_chips, centers):
    index = jnp.arange(SAMPLES, dtype=jnp.int32)
    chip_index = index * CHIPS // SAMPLES
    halves = 2 * index * CHIPS // SAMPLES % 2
    values = (jnp.take(code_chips, chip_index, axis=1) * (1 - 2 * halves)[None, :]).astype(
        jnp.float32
    )
    turns = centers[:, None] * index[None, :] % SAMPLES
    phase = turns.astype(jnp.float32) * (2.0 * math.pi / SAMPLES)
    count = code_chips.shape[0]
    mod_re = (values * jnp.cos(phase)).reshape(count, SPLIT, SAMPLES // SPLIT)
    mod_im = (values * jnp.sin(phase)).reshape(count, SPLIT, SAMPLES // SPLIT)
    return forward(mod_re, mod_im)


def power_rows(code_re, code_im, spectra, count_rows):
    sig_re = spectra[:, 0]
    sig_im = spectra[:, 1]
    sats = code_re.shape[0]
    count = sig_re.shape[0]
    prod_re = sig_re[None] * code_re[:, None] + sig_im[None] * code_im[:, None]
    prod_im = sig_im[None] * code_re[:, None] - sig_re[None] * code_im[:, None]
    shape = (sats * count, SPLIT, SAMPLES // SPLIT)
    out_re, out_im = inverse_rows(prod_re.reshape(shape), prod_im.reshape(shape))
    scaled_re = out_re * (1.0 / SAMPLES)
    scaled_im = out_im * (1.0 / SAMPLES)
    power = (scaled_re * scaled_re + scaled_im * scaled_im) / SAMPLES
    return power.reshape(sats, count, count_rows * (SAMPLES // SPLIT))


def power_maps(code_re, code_im, spectra):
    return power_rows(code_re, code_im, spectra, SPLIT)


def on_device(samples, code_chips, centers, widths):
    received = lax.all_gather(samples, SAT_DOP, axis=1, tiled=True)
    code_re, code_im = code_spectra(code_chips, centers)
    dop_rows = DOP // lax.axis_size(DOP_AXES)
    first = lax.axis_index(DOP_AXES) * dop_rows
    spectra = signal_spectra(received, first + jnp.arange(dop_rows, dtype=jnp.int32))
    power = power_maps(code_re, code_im, spectra)
    regrouped = core_and_chips(power, ("dop_0", "dop_1"), (1, 0), 2, 1)
    total = of_everyone(jnp.sum(regrouped, axis=(1, 2)), DOP_AXES)
    mean_power = total / (DOP * SAMPLES)
    rows = jnp.arange(DOP, dtype=jnp.int32)
    gap = jnp.abs(rows[:, None] - rows[None, :])
    band = ((gap[None] >= 2) & (gap[None] <= 1 + widths[:, None, None])).astype(jnp.float32)
    count = jnp.sum(band, axis=2)
    window = jnp.einsum("srq,sqt->srt", band, regrouped, precision=highest)
    noise = window / count[:, :, None]
    return regrouped / (noise + 0.25 * mean_power[:, None, None] + 1e-06)


def solution(mesh):
    split = Mesh(mesh.devices.reshape(mesh.shape["sat"], 4, 2), ("sat", "dop_0", "dop_1"))
    in_specs = (P(None, SAT_DOP), P("sat", None), P("sat"), P("sat"))
    out_specs = P("sat", None, DOP_AXES)
    return jax.shard_map(
        on_device, mesh=split, in_specs=in_specs, out_specs=out_specs, check_vma=False
    )
```

profile of v0, /device:TPU:1, one launch (start us, length us, event | category | flops | bytes accessed | tf_op | source)
XLA Modules:
  0.0 154.3 jit_solution(6594949316609923945)
XLA Ops:
  0.0 0.2 compare_select_fusion
  0.3 1.5 copy.42
  1.8 27.9 %gather_fusion = s32[8192,3]{1,0:T(8,128)} fusion(s32[3,4092]{0,1:T(8,128)S(1)} %copy.42, s32[8192]{0:T(1024)S(1)} %broadcast_clamp_fusion), kind=kCustom, calls=%fused_computation | custom fusion | bytes 229376 | tf_op jit(solution)/shard_map/jit(_take)/gather | solution.py:129
  29.7 2.9 %copy.43 = s32[3,64,128]{2,1,0:T(8,128)S(1)} copy(s32[3,64,128]{0,2,1:T(8,128)} %bitcast.94) | data formatting | bytes 196608 | tf_op jit(solution)/shard_map/jit(_take)/gather | solution.py:129
  32.5 0.0 copy-done.1
  32.6 0.8 fusion.69
  33.4 0.8 fusion.67
  34.2 0.1 fusion.95
  34.3 39.0 %all-gather = f32[128,64,2]{1,2,0:T(2,128)S(1)} all-gather(f32[1,64,2]{1,2,0:T(2,128)S(1)} %bitcast.106), channel_id=1, replica_groups=mesh['sat'=16,'dop_0'=4,'dop_1'=2] {'sat','dop_0','dop_1'}, dimensions={0}, use_global_device_ids=true | all-gather | bytes 66048 | tf_op jit(solution)/shard_map/all_gather | solution.py:160
  73.4 0.1 reshape.300
  73.5 0.1 fusion.235
  73.6 2.9 %fusion.12 = f32[16,128,64]{1,2,0:T(8,128)S(1)} fusion(f32[64,128]{1,0:T(8,128)S(1)} %bitcast.102, s32[64,128]{1,0:T(8,128)S(1)} %get-tuple-element.10, s32[16]{0:T(128)S(1)} %add_add_fusion, f32[64,128]{1,0:T(8,128)S(1)} %bitcast.98), kind=kOutput, calls=%fused_computation.38 | convolution fusion | flops 102948864 | bytes 622656 | tf_op jit(solution)/shard_map/kn,bnq->bkq/dot_general | solution.py:73
  76.4 2.9 %fusion.13 = f32[16,128,64]{1,2,0:T(8,128)S(1)} fusion(f32[64,128]{1,0:T(8,128)S(1)} %bitcast.103, s32[64,128]{1,0:T(8,128)S(1)} %get-tuple-element.10, s32[16]{0:T(128)S(1)} %add_add_fusion, f32[64,128]{1,0:T(8,128)S(1)} %bitcast.99), kind=kOutput, calls=%fused_computation.39 | convolution fusion | flops 102948864 | bytes 622656 | tf_op jit(solution)/shard_map/kn,bnq->bkq/dot_general | solution.py:73
  79.3 0.8 fusion.3
  80.2 0.8 fusion.2
  81.0 0.5 fusion.39
  81.5 0.5 fusion.42
  82.0 2.9 %fusion.1 = f32[16,64,128]{2,1,0:T(8,128)S(1)} fusion(f32[16,128,64]{1,2,0:T(8,128)S(1)} %fusion.12, f32[64,128]{1,0:T(8,128)S(1)} %bitcast.104, s32[64,128]{1,0:T(8,128)S(1)} %get-tuple-element.10, s32[16]{0:T(128)S(1)} %add_add_fusion, f32[64,128]{1,0:T(8,128)S(1)} %bitcast.100), kind=kOutput, calls=%fused_computation.14 | convolution fusion | flops 103079936 | bytes 1146944 | tf_op jit(solution)/shard_map/kn,bnq->bkq/dot_general | solution.py:73
  84.9 3.1 %fusion = f32[16,64,128]{2,1,0:T(8,128)S(1)} fusion(f32[16,128,64]{1,2,0:T(8,128)S(1)} %fusion.13, f32[64,128]{1,0:T(8,128)S(1)} %bitcast.105, s32[64,128]{1,0:T(8,128)S(1)} %get-tuple-element.10, s32[16]{0:T(128)S(1)} %add_add_fusion, f32[64,128]{1,0:T(8,128)S(1)} %bitcast.101), kind=kOutput, calls=%fused_computation.12 | convolution fusion | flops 103079936 | bytes 1146944 | tf_op jit(solution)/shard_map/kn,bnq->bkq/dot_general | solution.py:73
  88.0 0.8 fusion.19
  88.8 0.8 fusion.18
  89.6 0.5 convolution_subtract_fusion.3
  90.1 0.8 convolution_subtract_fusion.1
  91.0 0.5 convolution_add_fusion.3
  91.5 0.8 convolution_add_fusion.1
  92.3 0.5 multiply_subtract_fusion.1
  92.8 1.7 %fusion.37 = f32[48,64,128]{2,1,0:T(8,128)S(1)} fusion(f32[48,64,128]{2,1,0:T(8,128)S(1)} %bitcast.89), kind=kOutput, calls=%fused_computation.84 | convolution fusion | flops 604209152 | bytes 3145728 | tf_op jit(solution)/shard_map/bkn,nm->bkm/dot_general | solution.py:77
  94.5 1.7 %fusion.35 = f32[48,64,128]{2,1,0:T(8,128)S(1)} fusion(f32[48,64,128]{2,1,0:T(8,128)S(1)} %bitcast.91), kind=kOutput, calls=%fused_computation.82 | convolution fusion | flops 604209152 | bytes 3145728 | tf_op jit(solution)/shard_map/bkn,nm->bkm/dot_general | solution.py:77
  96.2 2.1 %convolution_subtract_fusion = f32[48,64,128]{2,1,0:T(8,128)S(1)} fusion(f32[48,64,128]{2,1,0:T(8,128)S(1)} %fusion.37, f32[48,64,128]{2,1,0:T(8,128)S(1)} %bitcast.92), kind=kOutput, calls=%fused_computation.8 | convolution fusion | flops 604602368 | bytes 4718592 | tf_op jit(solution)/shard_map/bkn,nm->bkm/dot_general | solution.py:77
  98.4 1.7 %convolution_add_fusion = f32[48,64,128]{2,1,0:T(8,128)S(1)} fusion(f32[48,64,128]{2,1,0:T(8,128)S(1)} %fusion.35, f32[48,64,128]{2,1,0:T(8,128)S(1)} %bitcast.90), kind=kOutput, calls=%fused_computation.7 | convolution fusion | flops 604602368 | bytes 4718592 | tf_op jit(solution)/shard_map/bkn,nm->bkm/dot_general | solution.py:77
  100.1 1.9 %fusion.8 = f32[48,128,64]{1,2,0:T(8,128)S(1)} fusion(f32[48,64,128]{2,1,0:T(8,128)S(1)} %convolution_subtract_fusion, f32[48,64,128]{2,1,0:T(8,128)S(1)} %convolution_add_fusion, f32[64,128]{1,0:T(8,128)S(1)} %get-tuple-element.11, f32[64,128]{1,0:T(8,128)S(1)} %get-tuple-element.12), kind=kOutput, calls=%fused_computation.34 | convolution fusion | flops 303226880 | bytes 4784128 | tf_op jit(solution)/shard_map/kn,bnq->bkq/dot_general | solution.py:73
  102.0 1.9 %fusion.7 = f32[48,128,64]{1,2,0:T(8,128)S(1)} fusion(f32[48,64,128]{2,1,0:T(8,128)S(1)} %convolution_add_fusion, f32[48,64,128]{2,1,0:T(8,128)S(1)} %convolution_subtract_fusion, f32[64,128]{1,0:T(8,128)S(1)} %get-tuple-element.11, f32[64,128]{1,0:T(8,128)S(1)} %get-tuple-element.12), kind=kOutput, calls=%fused_computation.33 | convolution fusion | flops 303226880 | bytes 4784128 | tf_op jit(solution)/shard_map/kn,bnq->bkq/dot_general | solution.py:73
  103.8 1.9 %fusion.9 = f32[48,128,64]{1,2,0:T(8,128)S(1)} fusion(f32[48,64,128]{2,1,0:T(8,128)S(1)} %convolution_subtract_fusion, f32[48,64,128]{2,1,0:T(8,128)S(1)} %convolution_add_fusion, f32[64,128]{1,0:T(8,128)S(1)} %get-tuple-element.11, f32[64,128]{1,0:T(8,128)S(1)} %get-tuple-element.12), kind=kOutput, calls=%fused_computation.35 | convolution fusion | flops 303226880 | bytes 4784128 | tf_op jit(solution)/shard_map/kn,bnq->bkq/dot_general | solution.py:73
  105.7 2.2 %multiply_bitcast_fusion = f32[48,64,128]{2,1,0:T(8,128)S(1)} fusion(f32[48,128,64]{1,2,0:T(8,128)S(1)} %fusion.8, f32[48,128,64]{1,2,0:T(8,128)S(1)} %fusion.7, f32[48,128,64]{1,2,0:T(8,128)S(1)} %fusion.9, f32[48,64,128]{2,1,0:T(8,128)S(1)} %convolution_add_fusion, f32[48,64,128]{2,1,0:T(8,128)S(1)} %convolution_subtract_fusion, ...), kind=kOutput, calls=%fused_computation.1 | convolution fusion | flops 306372608 | bytes 9502720 | tf_op jit(solution)/shard_map/kn,bnq->bkq/dot_general | solution.py:73
  107.9 0.2 reshape_reshape.3
  108.2 0.9 copy.44
  109.1 1.0 copy.45
  110.1 4.9 %all_to_all.16 = f32[4,2,3,16,1024]{4,0,3,2,1:T(4,128)S(1)} all-to-all(f32[4,2,3,16,1024]{4,0,3,2,1:T(4,128)S(1)} %copy.45), channel_id=1, replica_groups=mesh['sat'=16,'dop_0'=4,'dop_1'=2] {'dop_1'}, dimensions={1} | all-to-all | bytes 3145728 | tf_op jit(solution)/shard_map/all_to_all | solution.py:36
  115.1 2.4 %copy.46 = f32[4,2,3,16,1024]{4,1,3,2,0:T(2,128)} copy(f32[4,2,3,16,1024]{4,0,3,2,1:T(4,128)S(1)} %all_to_all.16) | data formatting | bytes 3145728 | tf_op jit(solution)/shard_map/all_to_all | solution.py:36
  117.4 3.7 %all-to-all-start.1 = ((f32[4,2,3,16,1024]{4,1,3,2,0:T(2,128)}), f32[4,2,3,16,1024]{4,1,3,2,0:T(2,128)S(1)}, u32[]{:S(2)}, u32[]{:S(2)}) async-start(f32[4,2,3,16,1024]{4,1,3,2,0:T(2,128)} %copy.46), calls=%async_computation.1 | async-start | bytes 3145728 | tf_op jit(solution)/shard_map/all_to_all | solution.py:36
  121.2 0.2 convert_reduce_fusion
  121.4 20.0 %all-to-all-done.1 = f32[4,2,3,16,1024]{4,1,3,2,0:T(2,128)S(1)} async-done(((f32[4,2,3,16,1024]{4,1,3,2,0:T(2,128)}), f32[4,2,3,16,1024]{4,1,3,2,0:T(2,128)S(1)}, u32[]{:S(2)}, u32[]{:S(2)}) %all-to-all-start.1) | async-done | bytes 1572896 | tf_op jit(solution)/shard_map/all_to_all | solution.py:36
  141.4 0.7 reduce_sum.28
  142.1 0.6 broadcast_in_dim.14
  142.7 4.6 %all-to-all-start.2 = ((f32[8,1,3]{2,1,0:T(1,128)}), f32[8,1,3]{2,1,0:T(1,128)S(1)}, u32[]{:S(2)}, u32[]{:S(2)}) async-start(f32[8,1,3]{2,1,0:T(1,128)} %broadcast_in_dim.14), calls=%async_computation.2 | async-start | bytes 8192 | tf_op jit(solution)/shard_map/all_to_all | solution.py:48
  147.2 0.5 copy.50
  147.7 4.1 %all-to-all-done.2 = f32[8,1,3]{2,1,0:T(1,128)S(1)} async-done(((f32[8,1,3]{2,1,0:T(1,128)}), f32[8,1,3]{2,1,0:T(1,128)S(1)}, u32[]{:S(2)}, u32[]{:S(2)}) %all-to-all-start.2) | async-done | bytes 128 | tf_op jit(solution)/shard_map/all_to_all | solution.py:48
  151.8 2.3 %add_divide_fusion = f32[3,128,1024]{2,1,0:T(8,128)} fusion(f32[3,128,1024]{2,1,0:T(8,128)S(1)} %bitcast.95, f32[3]{0:T(128)S(1)} %broadcast_multiply_fusion, f32[3,128]{1,0:T(4,128)S(1)} %convert_reduce_fusion, s32[128,128]{1,0:T(8,128)S(1)} %subtract_abs_fusion, s32[3]{0:T(128)S(1)} %broadcast_add_fusion, pred[128,128]{1,0:T(8,128)(4,1)S(1)} %broadcast_compare_fusion), kind=kOutput, calls=%fused_computation.2 | convolution fusion | flops 605650944 | bytes 3229208 | tf_op jit(solution)/shard_map/srq,sqt->srt/dot_general | solution.py:173
  (15 shorter events, 0.2 us)
Async XLA Ops:
  29.7 2.9 %copy-start.1 = (s32[3]{0:T(128)S(1)}, s32[3]{0:T(128)}, u32[]{:S(2)}) copy-start(s32[3]{0:T(128)} %param.6) | copy-start | bytes 40
  29.7 4.7 %copy-start = (f32[2,64]{1,0:T(2,128)S(1)}, f32[2,64]{1,0:T(2,128)}, u32[]{:S(2)}) copy-start(f32[2,64]{1,0:T(2,128)} %param.4) | copy-start | bytes 1540
  117.4 3.8 %copy-start.2 = (s32[3]{0:T(128)S(1)}, s32[3]{0:T(128)}, u32[]{:S(2)}) copy-start(s32[3]{0:T(128)} %param.7) | copy-start | bytes 40
  117.4 24.0 %all-to-all-start.1 = ((f32[4,2,3,16,1024]{4,1,3,2,0:T(2,128)}), f32[4,2,3,16,1024]{4,1,3,2,0:T(2,128)S(1)}, u32[]{:S(2)}, u32[]{:S(2)}) async-start(f32[4,2,3,16,1024]{4,1,3,2,0:T(2,128)} %copy.46), calls=%async_computation.1 | async-start | bytes 3145728 | tf_op jit(solution)/shard_map/all_to_all | solution.py:36
  142.7 9.1 %all-to-all-start.2 = ((f32[8,1,3]{2,1,0:T(1,128)}), f32[8,1,3]{2,1,0:T(1,128)S(1)}, u32[]{:S(2)}, u32[]{:S(2)}) async-start(f32[8,1,3]{2,1,0:T(1,128)} %broadcast_in_dim.14), calls=%async_computation.2 | async-start | bytes 8192 | tf_op jit(solution)/shard_map/all_to_all | solution.py:48
where the time goes:
time: 157 us; the launch traced here: 154 us
  blocking collectives  43.9 us (28%)
  local copies, waits for them, and re-layouts  38 us (24%)
  matrix products  37.6 us (24%)
  waiting for transfers between devices  24 us (15%)
  starting transfers between devices  8.27 us (5%)
  other arithmetic  1.88 us (1%)
    all_gather x1, blocking collectives, on_device(): received = lax.all_gather(samples, SAT_DOP, axis=1, tiled=True)  39 us
    gather x2, local copies, waits for them, and re-layouts, code_spectra(): jnp.take(code_chips, chip_index, axis=1) * (1 - 2 * halves)[None, :]  30.8 us
    dot_general x12, matrix products, left_mul(): return jnp.einsum('kn,bnq->bkq', table, block, precision=highest)  22.8 us
    all_to_all x1, waiting for transfers between devices, moved_by_axis(): result = lax.all_to_all(result, axes[k], k, k, tiled=True)  20 us
    dot_general x12, matrix products, right_mul(): return jnp.einsum('bkn,nm->bkm', block, table, precision=highest)  12.5 us
    all_to_all x1, blocking collectives, moved_by_axis(): result = lax.all_to_all(result, axes[k], k, k, tiled=True)  4.95 us
    all_to_all x1, starting transfers between devices, sent_to_all(): lax.all_to_all(jnp.broadcast_to(shard[None], (length, *shard.shape)), axi...  4.57 us
    all_to_all x1, waiting for transfers between devices, sent_to_all(): lax.all_to_all(jnp.broadcast_to(shard[None], (length, *shard.shape)), axi...  4.06 us
  transfers between devices with their start and end apart: 2, of which 2 were waited for; matrix products, arithmetic and copies ran while one was open for 0% of the time, Pallas kernels for 0%

commit v1 on v0

v1 whole, which is shorter than its diff:
```python
import functools
import math

import jax
import jax.numpy as jnp
import numpy as np
from jax import lax
from jax.experimental import pallas as pl
from jax.experimental.pallas import tpu as pltpu
from jax.sharding import PartitionSpec as P

N = 8192
CHIPS = 4092
DOP = 128
SATS = 3
KLO = 64
KHI = 128
THI = 8
F32 = jnp.float32
BF16 = jnp.bfloat16
MESH = pl.DeviceIdType.MESH


def split_np(table):
    table = np.asarray(table, np.float32)
    high = table.astype(jnp.bfloat16)
    low = (table - high.astype(np.float32)).astype(jnp.bfloat16)
    return high, low


def split(value):
    high = value.astype(BF16)
    low = (value - high.astype(F32)).astype(BF16)
    return high, low


def dot(left, right):
    return jnp.dot(left, right, preferred_element_type=F32)


def phase(turns):
    return np.cos(2 * np.pi * turns), np.sin(2 * np.pi * turns)


def build_tables():
    out = {}
    kappa = np.arange(-32, 96)
    order = np.concatenate([np.arange(0, 64, 2), np.arange(1, 64, 2)])
    cos, sin = phase(-(kappa[:, None] * order[None, :] % 64) / 64)
    high, low = split_np(np.concatenate([cos, sin], 0))
    out["code_first"] = np.concatenate([high, low], 1)
    lanes = np.arange(128)
    out["code_twiddle"] = np.stack(phase(-(kappa[:, None] * lanes[None, :] % N) / N)).astype(np.float32)
    cos, sin = phase((lanes[:, None] * lanes[None, :] % 128) / 128)
    high, low = split_np(np.block([[cos, -sin], [sin, cos]]))
    out["right"] = np.stack([high, low])
    high, low = split_np(np.block([[cos, sin], [-sin, cos]]))
    out["left"] = np.stack([high, low])
    rho = np.arange(-64, 192)
    device = np.arange(128)
    cos, sin = phase(-((device[:, None] // 2) * rho[None, :] % 128) / 128)
    columns = []
    for parity in range(2):
        keep = (device % 2 == parity)[:, None]
        columns += [cos * keep, sin * keep]
    high, low = split_np(np.concatenate(columns, 1))
    out["signal_first"] = np.stack([high, low])
    out["signal_twiddle"] = np.stack(phase(-(lanes[:, None] * rho[None, :] % (2 * N)) / (2 * N))).astype(np.float32)
    out["inverse"] = np.stack(phase((lanes[:, None] * lanes[None, :] % 128) / 128)).astype(np.float32)
    step = phase(np.broadcast_to(lanes[:, None], (128, 128)) / N)
    out["step"] = np.stack(step).astype(np.float32)
    block = np.arange(8)
    low_k = np.arange(KLO)
    turn = phase((block[:, None] * low_k[None, :] % 8) / 8)
    out["block"] = np.stack([np.broadcast_to(t[:, :, None], (8, KLO, 128)) for t in turn], 1).astype(np.float32) / N
    first = np.arange(256)[None, :] - 2 * np.arange(KLO)[:, None]
    out["window"] = ((first >= 0) & (first < 128)).astype(jnp.bfloat16)
    return out


NAMES = ["code_first", "code_twiddle", "right", "left", "signal_first", "signal_twiddle", "inverse", "step", "window"]


def gather_kernel(row_ref, out_ref, own_sem, send_sem, recv_sem):
    sat = lax.axis_index("sat")
    dop = lax.axis_index("dop")
    x, z = sat // 4, sat % 4
    me = sat * 8 + dop
    barrier = pltpu.get_barrier_semaphore()
    peers = []
    for step in range(1, 8):
        peers.append({"sat": sat, "dop": (dop + step) % 8})
    for step in range(1, 4):
        peers.append({"sat": x * 4 + (z + step) % 4, "dop": dop})
    for step in range(1, 4):
        peers.append({"sat": (x + step) % 4 * 4 + z, "dop": dop})
    for peer in peers:
        pl.semaphore_signal(barrier, inc=1, device_id=peer, device_id_type=MESH)
    own = pltpu.make_async_copy(row_ref, out_ref.at[pl.ds(me, 1)], own_sem)
    own.start()
    pl.semaphore_wait(barrier, 13)

    def exchange(first, size, start, targets, source):
        copies = []
        for i, peer in enumerate(targets):
            copies.append(
                pltpu.make_async_remote_copy(
                    src_ref=source,
                    dst_ref=out_ref.at[pl.ds(start, size)],
                    send_sem=send_sem.at[first + i],
                    recv_sem=recv_sem.at[first + i],
                    device_id=peer,
                    device_id_type=MESH,
                )
            )
            copies[-1].start()
        return copies

    first = exchange(0, 1, me, peers[:7], row_ref)
    own.wait()
    for copy in first:
        copy.wait()
    second = exchange(7, 8, sat * 8, peers[7:10], out_ref.at[pl.ds(sat * 8, 8)])
    for copy in second:
        copy.wait()
    third = exchange(10, 32, x * 32, peers[10:13], out_ref.at[pl.ds(x * 32, 32)])
    for copy in third:
        copy.wait()


def gathered(row):
    return pl.pallas_call(
        gather_kernel,
        out_shape=jax.ShapeDtypeStruct((128, 1, 128), F32),
        in_specs=[pl.BlockSpec(memory_space=pltpu.VMEM)],
        out_specs=pl.BlockSpec(memory_space=pltpu.VMEM),
        scratch_shapes=[
            pltpu.SemaphoreType.DMA,
            pltpu.SemaphoreType.DMA((13,)),
            pltpu.SemaphoreType.DMA((13,)),
        ],
        compiler_params=pltpu.CompilerParams(collective_id=0, has_side_effects=True),
        name="gather",
    )(row)


def code_part(centers_ref, chips_ref, block_ref, code_first, code_twiddle, right, chip_rows, spectrum, code):
    chip_rows[...] = jnp.zeros_like(chip_rows)
    for s in range(SATS):
        for a in range(32):
            width = 128 if a < 31 else CHIPS - 31 * 128
            chip_rows[pl.ds(s * 32 + a, 1), 0:width] = chips_ref[s : s + 1, a * 128 : a * 128 + width].astype(F32)
    rows = chip_rows[...]
    lane = lax.broadcasted_iota(jnp.int32, (96, 128), 1)
    index = lax.broadcasted_iota(jnp.int32, (96, 128), 0)
    turned = pltpu.roll(rows, 64, 1)
    above = pltpu.roll(turned, 1, 0)
    odd = jnp.where(lane < 64, above, turned)
    both = jnp.concatenate([odd, rows], 0).astype(BF16)
    sample = lax.broadcasted_iota(jnp.int32, (128, 128), 1)
    chip = lax.broadcasted_iota(jnp.int32, (128, 128), 0)
    kind = lax.broadcasted_iota(jnp.int32, (192, 128), 0) % 32 // 4
    replica = jnp.zeros((192, 128), F32)
    for i in range(8):
        shifted = sample + (7 - i)
        hit = chip == 60 + (shifted >> 1)
        sign = 1.0 - 2.0 * (shifted & 1).astype(F32)
        select = jnp.where(hit, sign, 0.0).astype(BF16)
        replica = jnp.where(kind == i, dot(both, select), replica)
    start = (lax.broadcasted_iota(jnp.int32, (192, 128), 0) < 96) & (
        lax.broadcasted_iota(jnp.int32, (192, 128), 0) % 4 == 0
    ) & (lax.broadcasted_iota(jnp.int32, (192, 128), 1) == 0)
    replica = jnp.where(start, pltpu.roll(replica, 127, 1), replica).astype(BF16)
    for s in range(SATS):
        part = jnp.concatenate([replica[s * 32 : s * 32 + 32], replica[96 + s * 32 : 128 + s * 32]], 0)
        stage = dot(code_first[...], jnp.concatenate([part, part], 0))
        re, im = stage[:128], stage[128:]
        cos, sin = code_twiddle[0], code_twiddle[1]
        turned = jnp.concatenate([re * cos - im * sin, im * cos + re * sin], 1)
        high, low = split(turned)
        spectrum[s] = dot(
            jnp.concatenate([high, low, high], 1),
            jnp.concatenate([right[0], right[0], right[1]], 0),
        )
    cos, sin = block_ref[0], block_ref[1]
    for s in range(SATS):
        shifted = pltpu.roll(spectrum[s], 96 + centers_ref[s], 0)[:KLO]
        re, im = shifted[:, :128], shifted[:, 128:]
        code[s, 0] = re * cos + im * sin
        code[s, 1] = re * sin - im * cos


def table_part(code, inverse, step, left_high, left_low):
    def group(g, _):
        at = pl.multiple_of(g * 16, 16)
        rows = pl.ds(at, 16)
        step_re, step_im = step[0, rows, :], step[1, rows, :]

        def one(k, carry):
            e_re, e_im = carry
            for s in range(SATS):
                c_re = code[s, 0, pl.ds(k, 1), :]
                c_im = code[s, 1, pl.ds(k, 1), :]
                m_re = e_re * c_re - e_im * c_im
                m_im = e_re * c_im + e_im * c_re
                into = pl.ds(pl.multiple_of(s * 128 + at, 16), 16)
                high, low = split(m_re)
                left_high[k, into, 0:128] = high
                left_low[k, into, 0:128] = low
                high, low = split(m_im)
                left_high[k, into, 128:256] = high
                left_low[k, into, 128:256] = low
            return e_re * step_re - e_im * step_im, e_re * step_im + e_im * step_re

        lax.fori_loop(0, KLO, one, (inverse[0, rows, :], inverse[1, rows, :]), unroll=4)
        return 0

    lax.fori_loop(0, 8, group, 0)


def signal_part(rows, left, signal_first, signal_twiddle):
    turned = rows.T
    high, low = split(turned)
    stage = dot(
        jnp.concatenate([high, low, high], 1),
        jnp.concatenate([signal_first[0], signal_first[0], signal_first[1]], 0),
    )
    re, im = [], []
    for parity in range(2):
        cos = stage[:, parity * 512 : parity * 512 + 256]
        sin = stage[:, parity * 512 + 256 : parity * 512 + 512]
        re.append(cos[:64] - sin[64:])
        im.append(sin[:64] + cos[64:])
    re, im = jnp.concatenate(re, 0), jnp.concatenate(im, 0)
    cos, sin = signal_twiddle[0], signal_twiddle[1]
    both = jnp.concatenate([re * cos - im * sin, im * cos + re * sin], 0)
    high, low = split(both)
    return dot(
        jnp.concatenate([left[0], left[1], left[0]], 1),
        jnp.concatenate([high, high, low], 0),
    )


def mean_part(signal, window, code, mean_ref):
    size = signal[0:128, :] * signal[0:128, :] + signal[128:256, :] * signal[128:256, :]
    high, low = split(size)
    under = lax.dot_general(
        jnp.concatenate([window[...], window[...]], 1),
        jnp.concatenate([high, low], 1),
        (((1,), (1,)), ((), ())),
        preferred_element_type=F32,
    )
    for s in range(SATS):
        re, im = code[s, 0], code[s, 1]
        total = jnp.sum(under * (re * re + im * im), axis=(0, 1), keepdims=True)
        mean_ref[s] = jnp.broadcast_to(total * (1.0 / (DOP * N)), (8, 128))


EIGHTH = math.sqrt(0.5)


def dft8(re, im):
    def add(a, b):
        return (a[0] + b[0], a[1] + b[1])

    def sub(a, b):
        return (a[0] - b[0], a[1] - b[1])

    def turn(a):
        return (-a[1], a[0])

    v = list(zip(re, im))

    def dft4(a, b, c, d):
        p, m = add(a, c), sub(a, c)
        q, n = add(b, d), turn(sub(b, d))
        return add(p, q), add(m, n), sub(p, q), sub(m, n)

    e = dft4(v[0], v[2], v[4], v[6])
    o = dft4(v[1], v[3], v[5], v[7])
    w1 = ((o[1][0] - o[1][1]) * EIGHTH, (o[1][0] + o[1][1]) * EIGHTH)
    w2 = turn(o[2])
    w3 = ((-o[3][0] - o[3][1]) * EIGHTH, (o[3][0] - o[3][1]) * EIGHTH)
    w = [o[0], w1, w2, w3]
    return [add(e[i], w[i]) for i in range(4)] + [sub(e[i], w[i]) for i in range(4)]


def main_part(signal, left_high, left_low, stage, total, power_ref):
    lane = lax.broadcasted_iota(jnp.int32, (256, 128), 1)
    for lam in range(8):
        for kap in range(8):
            k = lam + 8 * kap
            if k == 0:
                window = signal[:, 0:128]
            else:
                window = jnp.where(
                    lane < 128 - 2 * k,
                    pltpu.roll(signal[:, 0:128], 128 - 2 * k, 1),
                    pltpu.roll(signal[:, 128:256], 128 - 2 * k, 1),
                )
            high, low = split(window)

            def embedded(part):
                re, im = part[:128], part[128:]
                return jnp.concatenate([jnp.concatenate([re, im], 1), jnp.concatenate([-im, re], 1)], 0)

            high, low = embedded(high), embedded(low)
            m_high, m_low = left_high[k], left_low[k]
            stage[kap] = dot(
                jnp.concatenate([m_high, m_low, m_high], 1), jnp.concatenate([high, high, low], 0)
            )

        def chunk(c, _):
            rows = pl.ds(pl.multiple_of(c * 8, 8), 8)
            re = [stage[kap, rows, 0:128] for kap in range(8)]
            im = [stage[kap, rows, 128:256] for kap in range(8)]
            out = dft8(re, im)
            for t in range(8):
                a, b = out[t]
                angle = 2 * math.pi * (lam * t % 64) / 64
                cos, sin = math.cos(angle), math.sin(angle)
                if lam * t:
                    a, b = a * cos - b * sin, a * sin + b * cos
                if lam:
                    a = a + total[t, rows, 0:128]
                    b = b + total[t, rows, 128:256]
                if lam < 7:
                    total[t, rows, 0:128] = a
                    total[t, rows, 128:256] = b
                else:
                    power_ref[t, rows, :] = (a * a + b * b) * (1.0 / N)
            return 0

        lax.fori_loop(0, SATS * 16, chunk, 0, unroll=2)


def compute_kernel(
    centers_ref, rows_ref, chips_ref, block_ref, code_first, code_twiddle, right, left, signal_first, signal_twiddle,
    inverse, step, window, power_ref, mean_ref, chip_rows, spectrum, code, left_high, left_low, signal, stage, total,
):
    code_part(centers_ref, chips_ref, block_ref, code_first, code_twiddle, right, chip_rows, spectrum, code)
    table_part(code, inverse, step, left_high, left_low)
    signal[...] = signal_part(rows_ref[:, 0, :], left, signal_first, signal_twiddle)
    mean_part(signal, window, code, mean_ref)
    main_part(signal, left_high, left_low, stage, total, power_ref)


def vmem():
    return pl.BlockSpec(memory_space=pltpu.VMEM)


def computed(rows, chips, centers, block, tables):
    return pl.pallas_call(
        compute_kernel,
        out_shape=[
            jax.ShapeDtypeStruct((THI, SATS * 128, DOP), F32),
            jax.ShapeDtypeStruct((SATS, 8, 128), F32),
        ],
        in_specs=[pl.BlockSpec(memory_space=pltpu.SMEM)] + [vmem()] * (3 + len(tables)),
        out_specs=[vmem(), vmem()],
        scratch_shapes=[
            pltpu.VMEM((96, 128), F32),
            pltpu.VMEM((SATS, 128, 256), F32),
            pltpu.VMEM((SATS, 2, KLO, 128), F32),
            pltpu.VMEM((KLO, SATS * 128, 256), BF16),
            pltpu.VMEM((KLO, SATS * 128, 256), BF16),
            pltpu.VMEM((256, 256), F32),
            pltpu.VMEM((8, SATS * 128, 256), F32),
            pltpu.VMEM((THI, SATS * 128, 256), F32),
        ],
        compiler_params=pltpu.CompilerParams(vmem_limit_bytes=60 << 20),
        name="compute",
    )(centers, rows, chips, block, *tables)


def finish_kernel(widths_ref, power_ref, mean_ref, out_ref):
    s = pl.program_id(0)
    width = widths_ref[s]
    r = lax.broadcasted_iota(jnp.int32, (DOP, DOP), 0)
    q = lax.broadcasted_iota(jnp.int32, (DOP, DOP), 1)
    gap = jnp.abs(r - q)
    band = ((gap >= 2) & (gap <= 1 + width)).astype(F32)
    count = jnp.sum(band, axis=0, keepdims=True)
    scale = 1.0 / count
    band = band.astype(BF16)
    band = jnp.concatenate([band, band], 0)
    floor = mean_ref[0, 0:1, :] * 0.25 + 1e-6
    for t in range(THI):
        power = power_ref[t]
        high, low = split(power)
        around = dot(jnp.concatenate([high, low], 1), band)
        ratio = power / (around * scale + floor)
        out_ref[0, :, t * 128 : t * 128 + 128] = ratio.T


def finished(power, mean, widths):
    return pl.pallas_call(
        finish_kernel,
        grid=(SATS,),
        out_shape=jax.ShapeDtypeStruct((SATS, DOP, THI * 128), F32),
        in_specs=[
            pl.BlockSpec(memory_space=pltpu.SMEM),
            pl.BlockSpec((THI, 128, DOP), lambda s: (0, s, 0)),
            pl.BlockSpec((1, 8, 128), lambda s: (s, 0, 0)),
        ],
        out_specs=pl.BlockSpec((1, DOP, THI * 128), lambda s: (s, 0, 0)),
        name="finish",
    )(widths, power, mean)


def on_device(samples, code_chips, centers, widths):
    tables = build_tables()
    rows = gathered(samples.reshape(1, 1, 128))
    block = jnp.asarray(tables["block"])[lax.axis_index("dop")]
    power, mean = computed(rows, code_chips, centers, block, [jnp.asarray(tables[n]) for n in NAMES])
    return finished(power, mean, widths)


def solution(mesh):
    both = ("sat", "dop")
    return jax.shard_map(
        on_device,
        mesh=mesh,
        in_specs=(P(None, both), P("sat", None), P("sat"), P("sat")),
        out_specs=P("sat", None, "dop"),
        check_vma=False,
    )
```

time: 157 us -> 58.4 us (0.37)
  the two profiles are of different devices: /device:TPU:1 before, /device:TPU:0 now
where the time goes in v1:
time: 58.4 us; the launch traced here: 58.2 us
  Pallas kernels  55.4 us (95%)
  local copies, waits for them, and re-layouts  2.75 us (5%)
    pallas_call x1, Pallas kernels, computed(): pl.pallas_call(compute_kernel, out_shape=[jax.ShapeDtypeStruct((THI, SATS...  33.1 us
    pallas_call x1, Pallas kernels, gathered(): pl.pallas_call(gather_kernel, out_shape=jax.ShapeDtypeStruct((128, 1, 128...  18.4 us
    pallas_call x1, Pallas kernels, finished(): pl.pallas_call(finish_kernel, grid=(SATS,), out_shape=jax.ShapeDtypeStruc...  3.88 us
    squeeze x1, local copies, waits for them, and re-layouts, on_device(): block = jnp.asarray(tables['block'])[lax.axis_index('dop')]  1.48 us
    reshape x1, local copies, waits for them, and re-layouts, on_device(): rows = gathered(samples.reshape(1, 1, 128))  1.27 us

profile of v1, /device:TPU:0, one launch (start us, length us, event | category | flops | bytes accessed | tf_op | source)
XLA Modules:
  0.0 58.2 jit_solution(3212762181317756231)
XLA Ops:
  0.0 1.3 %reshape.3.row_ref = f32[1,1,128]{2,1,0:T(1,128)} reshape(f32[2,64]{1,0:T(2,128)} %param.14) | data formatting | bytes 1024 | tf_op jit(solution)/shard_map/reshape | solution.py:413
  1.3 18.4 %gather.1.rows_ref = f32[128,1,128]{2,1,0:T(1,128)} custom-call(f32[1,1,128]{2,1,0:T(1,128)} %reshape.3.row_ref), custom_call_target="tpu_custom_call" | custom-call | tf_op jit(solution)/shard_map/gather/pallas_call | solution.py:132
  19.7 1.5 %dynamic-slice_bitcast_fusion.block_ref = f32[2,64,128]{2,1,0:T(8,128)} fusion(f32[8,2,64,128]{3,2,1,0:T(8,128)} %constant.28.clone, s32[]{:T(128)S(6)} %select_n.3), kind=kLoop, calls=%fused_computation | loop fusion | bytes 131076 | tf_op jit(solution)/shard_map/squeeze | solution.py:414
  21.2 33.1 %compute.1 = (f32[8,384,128]{2,1,0:T(8,128)}, f32[3,8,128]{2,1,0:T(8,128)}) custom-call(s32[3]{0:T(128)} %centers_ref.1, f32[128,1,128]{2,1,0:T(1,128)} %gather.1.rows_ref, s32[3,4092]{1,0:T(4,128)} %chips_ref.1, f32[2,64,128]{2,1,0:T(8,128)} %dynamic-slice_bitcast_fusion.block_ref, bf16[256,128]{1,0:T(8,128)(2,1)} %constant.29.clone.code_first, ...), custom_call_target="tpu_custom_call" | custom-call | tf_op jit(solution)/shard_map/compute/pallas_call | solution.py:353
  54.3 3.9 %finish.1 = f32[3,128,1024]{2,1,0:T(8,128)} custom-call(s32[3]{0:T(128)} %widths_ref.1, f32[8,384,128]{2,1,0:T(8,128)} %get-tuple-element.7.power_ref, f32[3,8,128]{2,1,0:T(8,128)} %get-tuple-element.8.mean_ref), custom_call_target="tpu_custom_call" | custom-call | tf_op jit(solution)/shard_map/finish/pallas_call | solution.py:397

commit v2 on v1

--- a/solution.py
+++ b/solution.py
@@ -1,4 +1,3 @@
-import functools
 import math
 
 import jax
@@ -69,10 +68,6 @@
     out["inverse"] = np.stack(phase((lanes[:, None] * lanes[None, :] % 128) / 128)).astype(np.float32)
     step = phase(np.broadcast_to(lanes[:, None], (128, 128)) / N)
     out["step"] = np.stack(step).astype(np.float32)
-    block = np.arange(8)
-    low_k = np.arange(KLO)
-    turn = phase((block[:, None] * low_k[None, :] % 8) / 8)
-    out["block"] = np.stack([np.broadcast_to(t[:, :, None], (8, KLO, 128)) for t in turn], 1).astype(np.float32) / N
     first = np.arange(256)[None, :] - 2 * np.arange(KLO)[:, None]
     out["window"] = ((first >= 0) & (first < 128)).astype(jnp.bfloat16)
     return out
@@ -81,70 +76,15 @@
 NAMES = ["code_first", "code_twiddle", "right", "left", "signal_first", "signal_twiddle", "inverse", "step", "window"]
 
 
-def gather_kernel(row_ref, out_ref, own_sem, send_sem, recv_sem):
-    sat = lax.axis_index("sat")
-    dop = lax.axis_index("dop")
-    x, z = sat // 4, sat % 4
-    me = sat * 8 + dop
-    barrier = pltpu.get_barrier_semaphore()
-    peers = []
-    for step in range(1, 8):
-        peers.append({"sat": sat, "dop": (dop + step) % 8})
-    for step in range(1, 4):
-        peers.append({"sat": x * 4 + (z + step) % 4, "dop": dop})
-    for step in range(1, 4):
-        peers.append({"sat": (x + step) % 4 * 4 + z, "dop": dop})
-    for peer in peers:
-        pl.semaphore_signal(barrier, inc=1, device_id=peer, device_id_type=MESH)
-    own = pltpu.make_async_copy(row_ref, out_ref.at[pl.ds(me, 1)], own_sem)
-    own.start()
-    pl.semaphore_wait(barrier, 13)
-
-    def exchange(first, size, start, targets, source):
-        copies = []
-        for i, peer in enumerate(targets):
-            copies.append(
-                pltpu.make_async_remote_copy(
-                    src_ref=source,
-                    dst_ref=out_ref.at[pl.ds(start, size)],
-                    send_sem=send_sem.at[first + i],
-                    recv_sem=recv_sem.at[first + i],
-                    device_id=peer,
-                    device_id_type=MESH,
-                )
-            )
-            copies[-1].start()
-        return copies
-
-    first = exchange(0, 1, me, peers[:7], row_ref)
-    own.wait()
-    for copy in first:
-        copy.wait()
-    second = exchange(7, 8, sat * 8, peers[7:10], out_ref.at[pl.ds(sat * 8, 8)])
-    for copy in second:
-        copy.wait()
-    third = exchange(10, 32, x * 32, peers[10:13], out_ref.at[pl.ds(x * 32, 32)])
-    for copy in third:
-        copy.wait()
-
-
-def gathered(row):
-    return pl.pallas_call(
-        gather_kernel,
-        out_shape=jax.ShapeDtypeStruct((128, 1, 128), F32),
-        in_specs=[pl.BlockSpec(memory_space=pltpu.VMEM)],
-        out_specs=pl.BlockSpec(memory_space=pltpu.VMEM),
-        scratch_shapes=[
-            pltpu.SemaphoreType.DMA,
-            pltpu.SemaphoreType.DMA((13,)),
-            pltpu.SemaphoreType.DMA((13,)),
-        ],
-        compiler_params=pltpu.CompilerParams(collective_id=0, has_side_effects=True),
-        name="gather",
-    )(row)
-
-
-def code_part(centers_ref, chips_ref, block_ref, code_first, code_twiddle, right, chip_rows, spectrum, code):
+def eighth_turns(turns):
+    half = jnp.where(turns >= 4, -1.0, 1.0)
+    part = turns & 3
+    cos = jnp.where(part == 0, 1.0, jnp.where(part == 1, EIGHTH, jnp.where(part == 2, 0.0, -EIGHTH)))
+    sin = jnp.where(part == 0, 0.0, jnp.where(part == 2, 1.0, EIGHTH))
+    return cos * half, sin * half
+
+
+def code_part(centers_ref, chips_ref, dop, code_first, code_twiddle, right, chip_rows, spectrum, code):
     chip_rows[...] = jnp.zeros_like(chip_rows)
     for s in range(SATS):
         for a in range(32):
@@ -182,7 +122,8 @@
             jnp.concatenate([high, low, high], 1),
             jnp.concatenate([right[0], right[0], right[1]], 0),
         )
-    cos, sin = block_ref[0], block_ref[1]
+    cos, sin = eighth_turns(lax.broadcasted_iota(jnp.int32, (KLO, 128), 0) * dop & 7)
+    cos, sin = cos * (1.0 / N), sin * (1.0 / N)
     for s in range(SATS):
         shifted = pltpu.roll(spectrum[s], 96 + centers_ref[s], 0)[:KLO]
         re, im = shifted[:, :128], shifted[:, 128:]
@@ -190,7 +131,7 @@
         code[s, 1] = re * sin - im * cos
 
 
-def table_part(code, inverse, step, left_high, left_low):
+def table_part(code, inverse, step, left_high, left_low, first, last):
     def group(g, _):
         at = pl.multiple_of(g * 16, 16)
         rows = pl.ds(at, 16)
@@ -215,7 +156,7 @@
         lax.fori_loop(0, KLO, one, (inverse[0, rows, :], inverse[1, rows, :]), unroll=4)
         return 0
 
-    lax.fori_loop(0, 8, group, 0)
+    lax.fori_loop(first, last, group, 0)
 
 
 def signal_part(rows, left, signal_first, signal_twiddle):
@@ -285,80 +226,155 @@
     return [add(e[i], w[i]) for i in range(4)] + [sub(e[i], w[i]) for i in range(4)]
 
 
-def main_part(signal, left_high, left_low, stage, total, power_ref):
+def products(lam, signal, left_high, left_low, stage, kap):
+    k = lam + 8 * kap
     lane = lax.broadcasted_iota(jnp.int32, (256, 128), 1)
-    for lam in range(8):
+    shift = 128 - 2 * k
+    window = jnp.where(
+        lane < shift,
+        pltpu.roll(signal[:, 0:128], shift, 1),
+        pltpu.roll(signal[:, 128:256], shift, 1),
+    )
+    high, low = split(window)
+
+    def embedded(part):
+        re, im = part[:128], part[128:]
+        return jnp.concatenate([jnp.concatenate([re, im], 1), jnp.concatenate([-im, re], 1)], 0)
+
+    high, low = embedded(high), embedded(low)
+    m_high, m_low = left_high[k], left_low[k]
+    stage[kap] = dot(jnp.concatenate([m_high, m_low, m_high], 1), jnp.concatenate([high, high, low], 0))
+
+
+def combine(stage, total, row, power_ref=None, first=False):
+    rows = pl.ds(row, 8)
+    re = [stage[kap, rows, 0:128] for kap in range(8)]
+    im = [stage[kap, rows, 128:256] for kap in range(8)]
+    out = dft8(re, im)
+    for t in range(8):
+        a, b = out[t]
+        if not first:
+            c, d = total[t, rows, 0:128], total[t, rows, 128:256]
+            if t:
+                cos, sin = math.cos(math.pi * t / 32), math.sin(math.pi * t / 32)
+                c, d = c * cos - d * sin, c * sin + d * cos
+            a, b = a + c, b + d
+        if power_ref is None:
+            total[t, rows, 0:128] = a
+            total[t, rows, 128:256] = b
+        else:
+            power_ref[t, rows, :] = (a * a + b * b) * (1.0 / N)
+
+
+def main_part(signal, left_high, left_low, even, odd, total, power_ref):
+    def both(lam, fill, drain, **kind):
         for kap in range(8):
-            k = lam + 8 * kap
-            if k == 0:
-                window = signal[:, 0:128]
-            else:
-                window = jnp.where(
-                    lane < 128 - 2 * k,
-                    pltpu.roll(signal[:, 0:128], 128 - 2 * k, 1),
-                    pltpu.roll(signal[:, 128:256], 128 - 2 * k, 1),
+            products(lam, signal, left_high, left_low, fill, kap)
+            for g in range(6):
+                combine(drain, total, kap * 48 + g * 8, **kind)
+
+    for kap in range(8):
+        products(7, signal, left_high, left_low, odd, kap)
+    both(6, even, odd, first=True)
+
+    def pair(i, _):
+        lam = 5 - 2 * i
+        both(lam, odd, even)
+        both(lam - 1, even, odd)
+        return 0
+
+    lax.fori_loop(0, 3, pair, 0)
+
+    def last(c, _):
+        combine(even, total, pl.multiple_of(c * 8, 8), power_ref)
+        return 0
+
+    lax.fori_loop(0, SATS * 16, last, 0, unroll=2)
+
+
+def compute_kernel(centers_ref, samples_ref, chips_hbm, *refs):
+    count = len(NAMES)
+    hbm = dict(zip(NAMES, refs[:count]))
+    power_ref, mean_ref = refs[count : count + 2]
+    refs = refs[count + 2 :]
+    table = dict(zip(NAMES, refs[:count]))
+    (gathered, chips, chip_rows, spectrum, code, left_high, left_low, signal, even, odd, total,
+     own_sem, table_sem, send_sem, recv_sem) = refs[count:]
+    sat = lax.axis_index("sat")
+    dop = lax.axis_index("dop")
+    x, z = sat // 4, sat % 4
+    me = sat * 8 + dop
+    barrier = pltpu.get_barrier_semaphore()
+    peers = [{"sat": sat, "dop": (dop + step) % 8} for step in range(1, 8)]
+    peers += [{"sat": x * 4 + (z + step) % 4, "dop": dop} for step in range(1, 4)]
+    peers += [{"sat": (x + step) % 4 * 4 + z, "dop": dop} for step in range(1, 4)]
+    for peer in peers:
+        pl.semaphore_signal(barrier, inc=1, device_id=peer, device_id_type=MESH)
+    own = pltpu.make_async_copy(samples_ref, gathered.at[me], own_sem)
+    own.start()
+    loads = {"chips": pltpu.make_async_copy(chips_hbm, chips, table_sem.at[count])}
+    loads["chips"].start()
+    for i, name in enumerate(NAMES):
+        loads[name] = pltpu.make_async_copy(hbm[name], table[name], table_sem.at[i])
+        loads[name].start()
+
+    def exchange(first, size, start, targets, source):
+        copies = []
+        for i, peer in enumerate(targets):
+            copies.append(
+                pltpu.make_async_remote_copy(
+                    src_ref=source,
+                    dst_ref=gathered.at[pl.ds(start, size)],
+                    send_sem=send_sem.at[first + i],
+                    recv_sem=recv_sem.at[first + i],
+                    device_id=peer,
+                    device_id_type=MESH,
                 )
-            high, low = split(window)
-
-            def embedded(part):
-                re, im = part[:128], part[128:]
-                return jnp.concatenate([jnp.concatenate([re, im], 1), jnp.concatenate([-im, re], 1)], 0)
-
-            high, low = embedded(high), embedded(low)
-            m_high, m_low = left_high[k], left_low[k]
-            stage[kap] = dot(
-                jnp.concatenate([m_high, m_low, m_high], 1), jnp.concatenate([high, high, low], 0)
             )
-
-        def chunk(c, _):
-            rows = pl.ds(pl.multiple_of(c * 8, 8), 8)
-            re = [stage[kap, rows, 0:128] for kap in range(8)]
-            im = [stage[kap, rows, 128:256] for kap in range(8)]
-            out = dft8(re, im)
-            for t in range(8):
-                a, b = out[t]
-                angle = 2 * math.pi * (lam * t % 64) / 64
-                cos, sin = math.cos(angle), math.sin(angle)
-                if lam * t:
-                    a, b = a * cos - b * sin, a * sin + b * cos
-                if lam:
-                    a = a + total[t, rows, 0:128]
-                    b = b + total[t, rows, 128:256]
-                if lam < 7:
-                    total[t, rows, 0:128] = a
-                    total[t, rows, 128:256] = b
-                else:
-                    power_ref[t, rows, :] = (a * a + b * b) * (1.0 / N)
-            return 0
-
-        lax.fori_loop(0, SATS * 16, chunk, 0, unroll=2)
-
-
-def compute_kernel(
-    centers_ref, rows_ref, chips_ref, block_ref, code_first, code_twiddle, right, left, signal_first, signal_twiddle,
-    inverse, step, window, power_ref, mean_ref, chip_rows, spectrum, code, left_high, left_low, signal, stage, total,
-):
-    code_part(centers_ref, chips_ref, block_ref, code_first, code_twiddle, right, chip_rows, spectrum, code)
-    table_part(code, inverse, step, left_high, left_low)
-    signal[...] = signal_part(rows_ref[:, 0, :], left, signal_first, signal_twiddle)
-    mean_part(signal, window, code, mean_ref)
-    main_part(signal, left_high, left_low, stage, total, power_ref)
+            copies[-1].start()
+        return copies
+
+    own.wait()
+    pl.semaphore_wait(barrier, 13)
+    copies = exchange(0, 1, me, peers[:7], gathered.at[pl.ds(me, 1)])
+    for name in ("chips", "code_first", "code_twiddle", "right"):
+        loads[name].wait()
+    code_part(centers_ref, chips, dop, table["code_first"], table["code_twiddle"], table["right"], chip_rows, spectrum, code)
+    for copy in copies:
+        copy.wait()
+    copies = exchange(7, 8, sat * 8, peers[7:10], gathered.at[pl.ds(sat * 8, 8)])
+    for name in ("inverse", "step", "left", "signal_first", "signal_twiddle", "window"):
+        loads[name].wait()
+    table_part(code, table["inverse"], table["step"], left_high, left_low, 0, 3)
+    for copy in copies:
+        copy.wait()
+    copies = exchange(10, 32, x * 32, peers[10:13], gathered.at[pl.ds(x * 32, 32)])
+    table_part(code, table["inverse"], table["step"], left_high, left_low, 3, 8)
+    for copy in copies:
+        copy.wait()
+    rows = jnp.concatenate([gathered[:, 0, :], gathered[:, 1, :]], 1)
+    signal[...] = signal_part(rows, table["left"], table["signal_first"], table["signal_twiddle"])
+    mean_part(signal, table["window"], code, mean_ref)
+    main_part(signal, left_high, left_low, even, odd, total, power_ref)
 
 
 def vmem():
     return pl.BlockSpec(memory_space=pltpu.VMEM)
 
 
-def computed(rows, chips, centers, block, tables):
+def computed(samples, chips, centers, tables):
     return pl.pallas_call(
         compute_kernel,
         out_shape=[
             jax.ShapeDtypeStruct((THI, SATS * 128, DOP), F32),
             jax.ShapeDtypeStruct((SATS, 8, 128), F32),
         ],
-        in_specs=[pl.BlockSpec(memory_space=pltpu.SMEM)] + [vmem()] * (3 + len(tables)),
+        in_specs=[pl.BlockSpec(memory_space=pltpu.SMEM)] + [pl.BlockSpec(memory_space=pl.ANY)] * (2 + len(tables)),
         out_specs=[vmem(), vmem()],
-        scratch_shapes=[
+        scratch_shapes=[pltpu.VMEM(t.shape, t.dtype) for t in tables]
+        + [
+            pltpu.VMEM((128, 2, 64), F32),
+            pltpu.VMEM((SATS, CHIPS), jnp.int32),
             pltpu.VMEM((96, 128), F32),
             pltpu.VMEM((SATS, 128, 256), F32),
             pltpu.VMEM((SATS, 2, KLO, 128), F32),
@@ -366,11 +382,16 @@
             pltpu.VMEM((KLO, SATS * 128, 256), BF16),
             pltpu.VMEM((256, 256), F32),
             pltpu.VMEM((8, SATS * 128, 256), F32),
+            pltpu.VMEM((8, SATS * 128, 256), F32),
             pltpu.VMEM((THI, SATS * 128, 256), F32),
+            pltpu.SemaphoreType.DMA,
+            pltpu.SemaphoreType.DMA((len(tables) + 1,)),
+            pltpu.SemaphoreType.DMA((13,)),
+            pltpu.SemaphoreType.DMA((13,)),
         ],
-        compiler_params=pltpu.CompilerParams(vmem_limit_bytes=60 << 20),
+        compiler_params=pltpu.CompilerParams(vmem_limit_bytes=60 << 20, collective_id=0, has_side_effects=True),
         name="compute",
-    )(centers, rows, chips, block, *tables)
+    )(centers, samples, chips, *tables)
 
 
 def finish_kernel(widths_ref, power_ref, mean_ref, out_ref):
@@ -410,9 +431,7 @@
 
 def on_device(samples, code_chips, centers, widths):
     tables = build_tables()
-    rows = gathered(samples.reshape(1, 1, 128))
-    block = jnp.asarray(tables["block"])[lax.axis_index("dop")]
-    power, mean = computed(rows, code_chips, centers, block, [jnp.asarray(tables[n]) for n in NAMES])
+    power, mean = computed(samples, code_chips, centers, [jnp.asarray(tables[n]) for n in NAMES])
     return finished(power, mean, widths)
 
 

time: 58.4 us -> 41.9 us (0.72)
  the two profiles are of different devices: /device:TPU:0 before, /device:TPU:1 now
where the time goes in v2:
time: 41.9 us; the launch traced here: 41.7 us
  Pallas kernels  41.7 us (100%)
    pallas_call x1, Pallas kernels, computed(): pl.pallas_call(compute_kernel, out_shape=[jax.ShapeDtypeStruct((THI, SATS...  37.8 us
    pallas_call x1, Pallas kernels, finished(): pl.pallas_call(finish_kernel, grid=(SATS,), out_shape=jax.ShapeDtypeStruc...  3.9 us

profile of v2, /device:TPU:1, one launch (start us, length us, event | category | flops | bytes accessed | tf_op | source)
XLA Modules:
  0.0 41.7 jit_solution(15492290806584853131)
XLA Ops:
  0.0 37.8 %compute.1 = (f32[8,384,128]{2,1,0:T(8,128)}, f32[3,8,128]{2,1,0:T(8,128)}) custom-call(s32[3]{0:T(128)} %centers_ref.1, f32[2,64]{1,0:T(2,128)} %samples_ref.1, s32[3,4092]{1,0:T(4,128)} %chips_hbm.1, bf16[256,128]{1,0:T(8,128)(2,1)} %constant.18.clone.refs_0_, f32[2,128,128]{2,1,0:T(8,128)} %constant.19.clone.refs_1_, ...), custom_call_target="tpu_custom_call" | custom-call | tf_op jit(solution)/shard_map/compute/pallas_call | solution.py:366
  37.8 3.9 %finish.1 = f32[3,128,1024]{2,1,0:T(8,128)} custom-call(s32[3]{0:T(128)} %widths_ref.1, f32[8,384,128]{2,1,0:T(8,128)} %get-tuple-element.7.power_ref, f32[3,8,128]{2,1,0:T(8,128)} %get-tuple-element.8.mean_ref), custom_call_target="tpu_custom_call" | custom-call | tf_op jit(solution)/shard_map/finish/pallas_call | solution.py:418

commit v3 on v2

--- a/solution.py
+++ b/solution.py
@@ -232,8 +232,8 @@
     shift = 128 - 2 * k
     window = jnp.where(
         lane < shift,
-        pltpu.roll(signal[:, 0:128], shift, 1),
-        pltpu.roll(signal[:, 128:256], shift, 1),
+        pltpu.roll(signal[0:256, 0:128], shift, 1),
+        pltpu.roll(signal[0:256, 128:256], shift, 1),
     )
     high, low = split(window)
 
@@ -246,44 +246,51 @@
     stage[kap] = dot(jnp.concatenate([m_high, m_low, m_high], 1), jnp.concatenate([high, high, low], 0))
 
 
-def combine(stage, total, row, power_ref=None, first=False):
+def combine(stage, total, row, power_ref=None, pace=None):
     rows = pl.ds(row, 8)
     re = [stage[kap, rows, 0:128] for kap in range(8)]
     im = [stage[kap, rows, 128:256] for kap in range(8)]
     out = dft8(re, im)
     for t in range(8):
         a, b = out[t]
-        if not first:
-            c, d = total[t, rows, 0:128], total[t, rows, 128:256]
-            if t:
-                cos, sin = math.cos(math.pi * t / 32), math.sin(math.pi * t / 32)
-                c, d = c * cos - d * sin, c * sin + d * cos
-            a, b = a + c, b + d
+        c, d = total[t, rows, 0:128], total[t, rows, 128:256]
+        if t:
+            cos, sin = math.cos(math.pi * t / 32), math.sin(math.pi * t / 32)
+            c, d = c * cos - d * sin, c * sin + d * cos
+        a, b = a + c, b + d
         if power_ref is None:
             total[t, rows, 0:128] = a
             total[t, rows, 128:256] = b
         else:
             power_ref[t, rows, :] = (a * a + b * b) * (1.0 / N)
+    if pace is not None:
+        signal, spare = pace
+        signal[pl.ds(spare, 8), 0:128] = a
 
 
 def main_part(signal, left_high, left_low, even, odd, total, power_ref):
-    def both(lam, fill, drain, **kind):
+    def both(lam, fill, drain):
+        spare = pl.multiple_of(256 + 8 * (lam % 2), 8)
         for kap in range(8):
             products(lam, signal, left_high, left_low, fill, kap)
             for g in range(6):
-                combine(drain, total, kap * 48 + g * 8, **kind)
+                combine(drain, total, kap * 48 + g * 8, pace=(signal, spare))
 
     for kap in range(8):
         products(7, signal, left_high, left_low, odd, kap)
-    both(6, even, odd, first=True)
-
-    def pair(i, _):
-        lam = 5 - 2 * i
-        both(lam, odd, even)
-        both(lam - 1, even, odd)
+
+    def step(i, _):
+        @pl.when(i % 2 == 0)
+        def _():
+            both(6 - i, even, odd)
+
+        @pl.when(i % 2 == 1)
+        def _():
+            both(6 - i, odd, even)
+
         return 0
 
-    lax.fori_loop(0, 3, pair, 0)
+    lax.fori_loop(0, 7, step, 0)
 
     def last(c, _):
         combine(even, total, pl.multiple_of(c * 8, 8), power_ref)
@@ -306,8 +313,8 @@
     me = sat * 8 + dop
     barrier = pltpu.get_barrier_semaphore()
     peers = [{"sat": sat, "dop": (dop + step) % 8} for step in range(1, 8)]
-    peers += [{"sat": x * 4 + (z + step) % 4, "dop": dop} for step in range(1, 4)]
-    peers += [{"sat": (x + step) % 4 * 4 + z, "dop": dop} for step in range(1, 4)]
+    for step in range(1, 16):
+        peers.append({"sat": (x + step // 4) % 4 * 4 + (z + step % 4) % 4, "dop": dop})
     for peer in peers:
         pl.semaphore_signal(barrier, inc=1, device_id=peer, device_id_type=MESH)
     own = pltpu.make_async_copy(samples_ref, gathered.at[me], own_sem)
@@ -334,26 +341,24 @@
             copies[-1].start()
         return copies
 
-    own.wait()
-    pl.semaphore_wait(barrier, 13)
-    copies = exchange(0, 1, me, peers[:7], gathered.at[pl.ds(me, 1)])
     for name in ("chips", "code_first", "code_twiddle", "right"):
         loads[name].wait()
     code_part(centers_ref, chips, dop, table["code_first"], table["code_twiddle"], table["right"], chip_rows, spectrum, code)
-    for copy in copies:
-        copy.wait()
-    copies = exchange(7, 8, sat * 8, peers[7:10], gathered.at[pl.ds(sat * 8, 8)])
+    own.wait()
+    pl.semaphore_wait(barrier, 22)
+    copies = exchange(0, 1, me, peers[:7], gathered.at[pl.ds(me, 1)])
+    total[...] = jnp.zeros_like(total)
     for name in ("inverse", "step", "left", "signal_first", "signal_twiddle", "window"):
         loads[name].wait()
     table_part(code, table["inverse"], table["step"], left_high, left_low, 0, 3)
     for copy in copies:
         copy.wait()
-    copies = exchange(10, 32, x * 32, peers[10:13], gathered.at[pl.ds(x * 32, 32)])
+    copies = exchange(7, 8, sat * 8, peers[7:], gathered.at[pl.ds(sat * 8, 8)])
     table_part(code, table["inverse"], table["step"], left_high, left_low, 3, 8)
     for copy in copies:
         copy.wait()
     rows = jnp.concatenate([gathered[:, 0, :], gathered[:, 1, :]], 1)
-    signal[...] = signal_part(rows, table["left"], table["signal_first"], table["signal_twiddle"])
+    signal[0:256, :] = signal_part(rows, table["left"], table["signal_first"], table["signal_twiddle"])
     mean_part(signal, table["window"], code, mean_ref)
     main_part(signal, left_high, left_low, even, odd, total, power_ref)
 
@@ -369,7 +374,7 @@
             jax.ShapeDtypeStruct((THI, SATS * 128, DOP), F32),
             jax.ShapeDtypeStruct((SATS, 8, 128), F32),
         ],
-        in_specs=[pl.BlockSpec(memory_space=pltpu.SMEM)] + [pl.BlockSpec(memory_space=pl.ANY)] * (2 + len(tables)),
+        in_specs=[pl.BlockSpec(memory_space=pltpu.SMEM)] + [pl.BlockSpec(memory_space=pltpu.HBM)] * (2 + len(tables)),
         out_specs=[vmem(), vmem()],
         scratch_shapes=[pltpu.VMEM(t.shape, t.dtype) for t in tables]
         + [
@@ -380,58 +385,60 @@
             pltpu.VMEM((SATS, 2, KLO, 128), F32),
             pltpu.VMEM((KLO, SATS * 128, 256), BF16),
             pltpu.VMEM((KLO, SATS * 128, 256), BF16),
-            pltpu.VMEM((256, 256), F32),
+            pltpu.VMEM((272, 256), F32),
             pltpu.VMEM((8, SATS * 128, 256), F32),
             pltpu.VMEM((8, SATS * 128, 256), F32),
             pltpu.VMEM((THI, SATS * 128, 256), F32),
             pltpu.SemaphoreType.DMA,
             pltpu.SemaphoreType.DMA((len(tables) + 1,)),
-            pltpu.SemaphoreType.DMA((13,)),
-            pltpu.SemaphoreType.DMA((13,)),
+            pltpu.SemaphoreType.DMA((22,)),
+            pltpu.SemaphoreType.DMA((22,)),
         ],
-        compiler_params=pltpu.CompilerParams(vmem_limit_bytes=60 << 20, collective_id=0, has_side_effects=True),
+        compiler_params=pltpu.CompilerParams(vmem_limit_bytes=44 << 20, collective_id=0, has_side_effects=True),
         name="compute",
     )(centers, samples, chips, *tables)
 
 
-def finish_kernel(widths_ref, power_ref, mean_ref, out_ref):
-    s = pl.program_id(0)
-    width = widths_ref[s]
+def finish_kernel(widths_ref, power_ref, mean_ref, out_ref, ratios, sem):
     r = lax.broadcasted_iota(jnp.int32, (DOP, DOP), 0)
     q = lax.broadcasted_iota(jnp.int32, (DOP, DOP), 1)
     gap = jnp.abs(r - q)
-    band = ((gap >= 2) & (gap <= 1 + width)).astype(F32)
-    count = jnp.sum(band, axis=0, keepdims=True)
-    scale = 1.0 / count
-    band = band.astype(BF16)
-    band = jnp.concatenate([band, band], 0)
-    floor = mean_ref[0, 0:1, :] * 0.25 + 1e-6
-    for t in range(THI):
-        power = power_ref[t]
-        high, low = split(power)
-        around = dot(jnp.concatenate([high, low], 1), band)
-        ratio = power / (around * scale + floor)
-        out_ref[0, :, t * 128 : t * 128 + 128] = ratio.T
+    copies = []
+    for s in range(SATS):
+        band = ((gap >= 2) & (gap <= 1 + widths_ref[s])).astype(F32)
+        scale = 1.0 / jnp.sum(band, axis=0, keepdims=True)
+        band = band.astype(BF16)
+        band = jnp.concatenate([band, band], 0)
+        floor = mean_ref[s, 0:1, :] * 0.25 + 1e-6
+        for t in range(THI):
+            power = power_ref[t, s * 128 : s * 128 + 128, :]
+            high, low = split(power)
+            around = dot(jnp.concatenate([high, low], 1), band)
+            ratio = power / (around * scale + floor)
+            ratios[s, :, t * 128 : t * 128 + 128] = ratio.T
+        copies.append(pltpu.make_async_copy(ratios.at[s], out_ref.at[s], sem.at[s]))
+        copies[-1].start()
+    for copy in copies:
+        copy.wait()
 
 
 def finished(power, mean, widths):
     return pl.pallas_call(
         finish_kernel,
-        grid=(SATS,),
         out_shape=jax.ShapeDtypeStruct((SATS, DOP, THI * 128), F32),
-        in_specs=[
-            pl.BlockSpec(memory_space=pltpu.SMEM),
-            pl.BlockSpec((THI, 128, DOP), lambda s: (0, s, 0)),
-            pl.BlockSpec((1, 8, 128), lambda s: (s, 0, 0)),
-        ],
-        out_specs=pl.BlockSpec((1, DOP, THI * 128), lambda s: (s, 0, 0)),
+        in_specs=[pl.BlockSpec(memory_space=pltpu.SMEM), vmem(), vmem()],
+        out_specs=pl.BlockSpec(memory_space=pl.ANY),
+        scratch_shapes=[pltpu.VMEM((SATS, DOP, THI * 128), F32), pltpu.SemaphoreType.DMA((SATS,))],
+        compiler_params=pltpu.CompilerParams(vmem_limit_bytes=16 << 20),
         name="finish",
     )(widths, power, mean)
 
 
 def on_device(samples, code_chips, centers, widths):
     tables = build_tables()
-    power, mean = computed(samples, code_chips, centers, [jnp.asarray(tables[n]) for n in NAMES])
+    places = [samples, code_chips] + [jnp.asarray(tables[n]) for n in NAMES]
+    places = [pltpu.with_memory_space_constraint(a, pltpu.HBM) for a in places]
+    power, mean = computed(places[0], places[1], centers, places[2:])
     return finished(power, mean, widths)
 
 

time: 41.9 us -> 38.5 us (0.919)
  Pallas kernels: 41.7 us -> 37.7 us
  local copies, waits for them, and re-layouts: 0 us -> 0.66 us
    pallas_call x1, Pallas kernels: 37.8 us -> 35.6 us  [computed(): pl.pallas_call(compute_kernel, out_shape=[jax.ShapeDtypeStruct((THI, SATS...]
    pallas_call x1, Pallas kernels: 3.9 us -> 2.11 us  [finished(): pl.pallas_call(finish_kernel, out_shape=jax.ShapeDtypeStruct((SATS, DOP,...]
    unnamed x0 -> x4, local copies, waits for them, and re-layouts: none -> 0.66 us
where the time goes in v3:
time: 38.5 us; the launch traced here: 38.4 us
  Pallas kernels  37.7 us (98%)
  local copies, waits for them, and re-layouts  0.66 us (2%)
    pallas_call x1, Pallas kernels, computed(): pl.pallas_call(compute_kernel, out_shape=[jax.ShapeDtypeStruct((THI, SATS...  35.6 us
    pallas_call x1, Pallas kernels, finished(): pl.pallas_call(finish_kernel, out_shape=jax.ShapeDtypeStruct((SATS, DOP,...  2.11 us

profile of v3, /device:TPU:1, one launch (start us, length us, event | category | flops | bytes accessed | tf_op | source)
XLA Modules:
  0.0 38.4 jit_solution(7958521680124269432)
XLA Ops:
  0.0 0.0 copy-start
  0.0 0.7 %copy-done = s32[3]{0:T(128)S(1)} copy-done((s32[3]{0:T(128)S(1)}, s32[3]{0:T(128)}, u32[]{:S(2)}) %copy-start) | copy-done | bytes 36
  0.7 0.0 copy-start.1
  0.7 35.6 %compute.1 = (f32[8,384,128]{2,1,0:T(8,128)S(1)}, f32[3,8,128]{2,1,0:T(8,128)S(1)}) custom-call(s32[3]{0:T(128)S(1)} %copy-done, f32[2,64]{1,0:T(2,128)} %samples_ref.1, s32[3,4092]{1,0:T(4,128)} %chips_hbm.1, bf16[256,128]{1,0:T(8,128)(2,1)} %constant.18.clone.refs_0_, f32[2,128,128]{2,1,0:T(8,128)} %constant.19.clone.refs_1_, ...), custom_call_target="tpu_custom_call" | custom-call | tf_op jit(solution)/shard_map/compute/pallas_call | solution.py:371
  36.2 0.0 copy-done.1
  36.2 2.1 %finish.1 = f32[3,128,1024]{2,1,0:T(8,128)} custom-call(s32[3]{0:T(128)S(1)} %copy-done.1, f32[8,384,128]{2,1,0:T(8,128)S(1)} %get-tuple-element.7.power_ref, f32[3,8,128]{2,1,0:T(8,128)S(1)} %get-tuple-element.8.mean_ref), custom_call_target="tpu_custom_call" | custom-call | tf_op jit(solution)/shard_map/finish/pallas_call | solution.py:426
Async XLA Ops:
  0.0 0.7 %copy-start = (s32[3]{0:T(128)S(1)}, s32[3]{0:T(128)}, u32[]{:S(2)}) copy-start(s32[3]{0:T(128)} %centers_ref.1) | copy-start | bytes 40
  0.7 35.6 %copy-start.1 = (s32[3]{0:T(128)S(1)}, s32[3]{0:T(128)}, u32[]{:S(2)}) copy-start(s32[3]{0:T(128)} %widths_ref.1) | copy-start | bytes 40

commit v4 on v3

--- a/solution.py
+++ b/solution.py
@@ -341,20 +341,20 @@
             copies[-1].start()
         return copies
 
+    own.wait()
+    pl.semaphore_wait(barrier, 22)
+    copies = exchange(0, 1, me, peers[:7], gathered.at[pl.ds(me, 1)])
     for name in ("chips", "code_first", "code_twiddle", "right"):
         loads[name].wait()
     code_part(centers_ref, chips, dop, table["code_first"], table["code_twiddle"], table["right"], chip_rows, spectrum, code)
-    own.wait()
-    pl.semaphore_wait(barrier, 22)
-    copies = exchange(0, 1, me, peers[:7], gathered.at[pl.ds(me, 1)])
-    total[...] = jnp.zeros_like(total)
     for name in ("inverse", "step", "left", "signal_first", "signal_twiddle", "window"):
         loads[name].wait()
-    table_part(code, table["inverse"], table["step"], left_high, left_low, 0, 3)
+    table_part(code, table["inverse"], table["step"], left_high, left_low, 0, 1)
     for copy in copies:
         copy.wait()
     copies = exchange(7, 8, sat * 8, peers[7:], gathered.at[pl.ds(sat * 8, 8)])
-    table_part(code, table["inverse"], table["step"], left_high, left_low, 3, 8)
+    total[...] = jnp.zeros_like(total)
+    table_part(code, table["inverse"], table["step"], left_high, left_low, 1, 8)
     for copy in copies:
         copy.wait()
     rows = jnp.concatenate([gathered[:, 0, :], gathered[:, 1, :]], 1)

time: 38.5 us -> 40.8 us (1.060)
  Pallas kernels: 37.7 us -> 40 us
    pallas_call x1, Pallas kernels: 35.6 us -> 37.9 us  [computed(): pl.pallas_call(compute_kernel, out_shape=[jax.ShapeDtypeStruct((THI, SATS...]
where the time goes in v4:
time: 40.8 us; the launch traced here: 40.7 us
  Pallas kernels  40 us (98%)
  local copies, waits for them, and re-layouts  0.66 us (2%)
    pallas_call x1, Pallas kernels, computed(): pl.pallas_call(compute_kernel, out_shape=[jax.ShapeDtypeStruct((THI, SATS...  37.9 us
    pallas_call x1, Pallas kernels, finished(): pl.pallas_call(finish_kernel, out_shape=jax.ShapeDtypeStruct((SATS, DOP,...  2.11 us

profile of v4, /device:TPU:1, one launch (start us, length us, event | category | flops | bytes accessed | tf_op | source)
XLA Modules:
  0.0 40.7 jit_solution(11754630318583438190)
XLA Ops:
  0.0 0.0 copy-start
  0.0 0.7 %copy-done = s32[3]{0:T(128)S(1)} copy-done((s32[3]{0:T(128)S(1)}, s32[3]{0:T(128)}, u32[]{:S(2)}) %copy-start) | copy-done | bytes 36
  0.7 0.0 copy-start.1
  0.7 37.9 %compute.1 = (f32[8,384,128]{2,1,0:T(8,128)S(1)}, f32[3,8,128]{2,1,0:T(8,128)S(1)}) custom-call(s32[3]{0:T(128)S(1)} %copy-done, f32[2,64]{1,0:T(2,128)} %samples_ref.1, s32[3,4092]{1,0:T(4,128)} %chips_hbm.1, bf16[256,128]{1,0:T(8,128)(2,1)} %constant.18.clone.refs_0_, f32[2,128,128]{2,1,0:T(8,128)} %constant.19.clone.refs_1_, ...), custom_call_target="tpu_custom_call" | custom-call | tf_op jit(solution)/shard_map/compute/pallas_call | solution.py:371
  38.6 0.0 copy-done.1
  38.6 2.1 %finish.1 = f32[3,128,1024]{2,1,0:T(8,128)} custom-call(s32[3]{0:T(128)S(1)} %copy-done.1, f32[8,384,128]{2,1,0:T(8,128)S(1)} %get-tuple-element.7.power_ref, f32[3,8,128]{2,1,0:T(8,128)S(1)} %get-tuple-element.8.mean_ref), custom_call_target="tpu_custom_call" | custom-call | tf_op jit(solution)/shard_map/finish/pallas_call | solution.py:426
Async XLA Ops:
  0.0 0.7 %copy-start = (s32[3]{0:T(128)S(1)}, s32[3]{0:T(128)}, u32[]{:S(2)}) copy-start(s32[3]{0:T(128)} %centers_ref.1) | copy-start | bytes 40
  0.7 37.9 %copy-start.1 = (s32[3]{0:T(128)S(1)}, s32[3]{0:T(128)}, u32[]{:S(2)}) copy-start(s32[3]{0:T(128)} %widths_ref.1) | copy-start | bytes 40

commit v5 on v3

--- a/solution.py
+++ b/solution.py
@@ -122,16 +122,18 @@
             jnp.concatenate([high, low, high], 1),
             jnp.concatenate([right[0], right[0], right[1]], 0),
         )
-    cos, sin = eighth_turns(lax.broadcasted_iota(jnp.int32, (KLO, 128), 0) * dop & 7)
-    cos, sin = cos * (1.0 / N), sin * (1.0 / N)
+    row = lax.broadcasted_iota(jnp.int32, (KLO, 128), 0)
     for s in range(SATS):
+        block = dop if s == 2 else dop // 2 * 2
+        cos, sin = eighth_turns(row * block & 7)
+        cos, sin = cos * (1.0 / N), sin * (1.0 / N)
         shifted = pltpu.roll(spectrum[s], 96 + centers_ref[s], 0)[:KLO]
-        re, im = shifted[:, :128], shifted[:, 128:]
+        re, im = shifted[:, :128], shifted[:, 128:256]
         code[s, 0] = re * cos + im * sin
         code[s, 1] = re * sin - im * cos
 
 
-def table_part(code, inverse, step, left_high, left_low, first, last):
+def table_part(code, own, inverse, step, left_high, left_low, first, last):
     def group(g, _):
         at = pl.multiple_of(g * 16, 16)
         rows = pl.ds(at, 16)
@@ -139,12 +141,12 @@
 
         def one(k, carry):
             e_re, e_im = carry
-            for s in range(SATS):
+            for slot, s in ((0, own), (1, 2)):
                 c_re = code[s, 0, pl.ds(k, 1), :]
                 c_im = code[s, 1, pl.ds(k, 1), :]
                 m_re = e_re * c_re - e_im * c_im
                 m_im = e_re * c_im + e_im * c_re
-                into = pl.ds(pl.multiple_of(s * 128 + at, 16), 16)
+                into = pl.ds(pl.multiple_of(slot * 128 + at, 16), 16)
                 high, low = split(m_re)
                 left_high[k, into, 0:128] = high
                 left_low[k, into, 0:128] = low
@@ -246,35 +248,33 @@
     stage[kap] = dot(jnp.concatenate([m_high, m_low, m_high], 1), jnp.concatenate([high, high, low], 0))
 
 
-def combine(stage, total, row, power_ref=None, pace=None):
+def combine(stage, total, slot, row, store=None):
     rows = pl.ds(row, 8)
-    re = [stage[kap, rows, 0:128] for kap in range(8)]
-    im = [stage[kap, rows, 128:256] for kap in range(8)]
+    from_rows = pl.ds(slot * 128 + row, 8)
+    re = [stage[kap, from_rows, 0:128] for kap in range(8)]
+    im = [stage[kap, from_rows, 128:256] for kap in range(8)]
     out = dft8(re, im)
-    for t in range(8):
-        a, b = out[t]
+    for t in range(total.shape[0]):
+        a, b = out[t % 8]
         c, d = total[t, rows, 0:128], total[t, rows, 128:256]
         if t:
             cos, sin = math.cos(math.pi * t / 32), math.sin(math.pi * t / 32)
             c, d = c * cos - d * sin, c * sin + d * cos
         a, b = a + c, b + d
-        if power_ref is None:
+        if store is None:
             total[t, rows, 0:128] = a
             total[t, rows, 128:256] = b
         else:
-            power_ref[t, rows, :] = (a * a + b * b) * (1.0 / N)
-    if pace is not None:
-        signal, spare = pace
-        signal[pl.ds(spare, 8), 0:128] = a
-
-
-def main_part(signal, left_high, left_low, even, odd, total, power_ref):
+            store(t, rows, (a * a + b * b) * (1.0 / N))
+
+
+def main_part(signal, left_high, left_low, even, odd, wide, narrow, power_ref, own, send):
     def both(lam, fill, drain):
-        spare = pl.multiple_of(256 + 8 * (lam % 2), 8)
         for kap in range(8):
             products(lam, signal, left_high, left_low, fill, kap)
-            for g in range(6):
-                combine(drain, total, kap * 48 + g * 8, pace=(signal, spare))
+            for g in range(2):
+                combine(drain, wide, 0, kap * 16 + g * 8)
+                combine(drain, narrow, 1, kap * 16 + g * 8)
 
     for kap in range(8):
         products(7, signal, left_high, left_low, odd, kap)
@@ -291,12 +291,37 @@
         return 0
 
     lax.fori_loop(0, 7, step, 0)
-
-    def last(c, _):
-        combine(even, total, pl.multiple_of(c * 8, 8), power_ref)
-        return 0
-
-    lax.fori_loop(0, SATS * 16, last, 0, unroll=2)
+    places = [jnp.where(own == half, own, 3) for half in range(2)]
+
+    def keep_wide(t, rows, value):
+        power_ref[places[t // 8], t % 8, rows, :] = value
+
+    def keep_narrow(t, rows, value):
+        power_ref[2, t, rows, :] = value
+
+    def finish_wide(first, last):
+        def one(c, _):
+            combine(even, wide, 0, pl.multiple_of(c * 8, 8), keep_wide)
+            return 0
+
+        lax.fori_loop(first, last, one, 0)
+
+    def finish_narrow(first, last):
+        def one(c, _):
+            combine(even, narrow, 1, pl.multiple_of(c * 8, 8), keep_narrow)
+            return 0
+
+        lax.fori_loop(first, last, one, 0, unroll=2)
+
+    finish_wide(0, 8)
+    finish_narrow(0, 4)
+    copies = [send(0)]
+    finish_wide(8, 16)
+    finish_narrow(4, 8)
+    copies.append(send(1))
+    finish_narrow(8, 16)
+    for copy in copies:
+        copy.wait()
 
 
 def compute_kernel(centers_ref, samples_ref, chips_hbm, *refs):
@@ -305,12 +330,13 @@
     power_ref, mean_ref = refs[count : count + 2]
     refs = refs[count + 2 :]
     table = dict(zip(NAMES, refs[:count]))
-    (gathered, chips, chip_rows, spectrum, code, left_high, left_low, signal, even, odd, total,
+    (gathered, chips, chip_rows, spectrum, code, left_high, left_low, signal, even, odd, wide, narrow,
      own_sem, table_sem, send_sem, recv_sem) = refs[count:]
     sat = lax.axis_index("sat")
     dop = lax.axis_index("dop")
     x, z = sat // 4, sat % 4
     me = sat * 8 + dop
+    own_sat = dop % 2
     barrier = pltpu.get_barrier_semaphore()
     peers = [{"sat": sat, "dop": (dop + step) % 8} for step in range(1, 8)]
     for step in range(1, 16):
@@ -347,20 +373,35 @@
     own.wait()
     pl.semaphore_wait(barrier, 22)
     copies = exchange(0, 1, me, peers[:7], gathered.at[pl.ds(me, 1)])
-    total[...] = jnp.zeros_like(total)
+    wide[...] = jnp.zeros_like(wide)
+    narrow[...] = jnp.zeros_like(narrow)
     for name in ("inverse", "step", "left", "signal_first", "signal_twiddle", "window"):
         loads[name].wait()
-    table_part(code, table["inverse"], table["step"], left_high, left_low, 0, 3)
+    table_part(code, own_sat, table["inverse"], table["step"], left_high, left_low, 0, 3)
     for copy in copies:
         copy.wait()
     copies = exchange(7, 8, sat * 8, peers[7:], gathered.at[pl.ds(sat * 8, 8)])
-    table_part(code, table["inverse"], table["step"], left_high, left_low, 3, 8)
+    table_part(code, own_sat, table["inverse"], table["step"], left_high, left_low, 3, 8)
     for copy in copies:
         copy.wait()
     rows = jnp.concatenate([gathered[:, 0, :], gathered[:, 1, :]], 1)
-    signal[0:256, :] = signal_part(rows, table["left"], table["signal_first"], table["signal_twiddle"])
+    signal[...] = signal_part(rows, table["left"], table["signal_first"], table["signal_twiddle"])
     mean_part(signal, table["window"], code, mean_ref)
-    main_part(signal, left_high, left_low, even, odd, total, power_ref)
+
+    def send(half):
+        rows = pl.ds(half * 64, 64)
+        copy = pltpu.make_async_remote_copy(
+            src_ref=power_ref.at[3, :, rows],
+            dst_ref=power_ref.at[own_sat, :, rows],
+            send_sem=send_sem.at[22 + half],
+            recv_sem=recv_sem.at[22 + half],
+            device_id={"sat": sat, "dop": dop + 1 - 2 * own_sat},
+            device_id_type=MESH,
+        )
+        copy.start()
+        return copy
+
+    main_part(signal, left_high, left_low, even, odd, wide, narrow, power_ref, own_sat, send)
 
 
 def vmem():
@@ -371,7 +412,7 @@
     return pl.pallas_call(
         compute_kernel,
         out_shape=[
-            jax.ShapeDtypeStruct((THI, SATS * 128, DOP), F32),
+            jax.ShapeDtypeStruct((SATS + 1, THI, 128, DOP), F32),
             jax.ShapeDtypeStruct((SATS, 8, 128), F32),
         ],
         in_specs=[pl.BlockSpec(memory_space=pltpu.SMEM)] + [pl.BlockSpec(memory_space=pltpu.HBM)] * (2 + len(tables)),
@@ -383,18 +424,19 @@
             pltpu.VMEM((96, 128), F32),
             pltpu.VMEM((SATS, 128, 256), F32),
             pltpu.VMEM((SATS, 2, KLO, 128), F32),
-            pltpu.VMEM((KLO, SATS * 128, 256), BF16),
-            pltpu.VMEM((KLO, SATS * 128, 256), BF16),
-            pltpu.VMEM((272, 256), F32),
-            pltpu.VMEM((8, SATS * 128, 256), F32),
-            pltpu.VMEM((8, SATS * 128, 256), F32),
-            pltpu.VMEM((THI, SATS * 128, 256), F32),
+            pltpu.VMEM((KLO, 256, 256), BF16),
+            pltpu.VMEM((KLO, 256, 256), BF16),
+            pltpu.VMEM((256, 256), F32),
+            pltpu.VMEM((8, 256, 256), F32),
+            pltpu.VMEM((8, 256, 256), F32),
+            pltpu.VMEM((2 * THI, 128, 256), F32),
+            pltpu.VMEM((THI, 128, 256), F32),
             pltpu.SemaphoreType.DMA,
             pltpu.SemaphoreType.DMA((len(tables) + 1,)),
-            pltpu.SemaphoreType.DMA((22,)),
-            pltpu.SemaphoreType.DMA((22,)),
+            pltpu.SemaphoreType.DMA((24,)),
+            pltpu.SemaphoreType.DMA((24,)),
         ],
-        compiler_params=pltpu.CompilerParams(vmem_limit_bytes=44 << 20, collective_id=0, has_side_effects=True),
+        compiler_params=pltpu.CompilerParams(vmem_limit_bytes=40 << 20, collective_id=0, has_side_effects=True),
         name="compute",
     )(centers, samples, chips, *tables)
 
@@ -411,7 +453,7 @@
         band = jnp.concatenate([band, band], 0)
         floor = mean_ref[s, 0:1, :] * 0.25 + 1e-6
         for t in range(THI):
-            power = power_ref[t, s * 128 : s * 128 + 128, :]
+            power = power_ref[s, t]
             high, low = split(power)
             around = dot(jnp.concatenate([high, low], 1), band)
             ratio = power / (around * scale + floor)

time: 38.5 us -> 36 us (0.935)
  Pallas kernels: 37.7 us -> 34.5 us
  local copies, waits for them, and re-layouts: 0.66 us -> 1.31 us
    pallas_call x1, Pallas kernels: 35.6 us -> 32.4 us  [computed(): pl.pallas_call(compute_kernel, out_shape=[jax.ShapeDtypeStruct((SATS + 1,...]
    unnamed x4, local copies, waits for them, and re-layouts: 0.66 us -> 1.31 us
where the time goes in v5:
time: 36 us; the launch traced here: 35.9 us
  Pallas kernels  34.5 us (96%)
  local copies, waits for them, and re-layouts  1.31 us (4%)
    pallas_call x1, Pallas kernels, computed(): pl.pallas_call(compute_kernel, out_shape=[jax.ShapeDtypeStruct((SATS + 1,...  32.4 us
    pallas_call x1, Pallas kernels, finished(): pl.pallas_call(finish_kernel, out_shape=jax.ShapeDtypeStruct((SATS, DOP,...  2.12 us
    unnamed x4, local copies, waits for them, and re-layouts  1.31 us

profile of v5, /device:TPU:1, one launch (start us, length us, event | category | flops | bytes accessed | tf_op | source)
XLA Modules:
  0.0 35.9 jit_solution(2267280140273346261)
XLA Ops:
  0.0 0.0 copy-start.1
  0.0 0.7 %copy-done.1 = s32[3]{0:T(128)S(1)} copy-done((s32[3]{0:T(128)S(1)}, s32[3]{0:T(128)}, u32[]{:S(2)}) %copy-start.1) | copy-done | bytes 36
  0.7 32.4 %compute.1 = (f32[4,8,128,128]{3,2,1,0:T(8,128)S(1)}, f32[3,8,128]{2,1,0:T(8,128)S(1)}) custom-call(s32[3]{0:T(128)S(1)} %copy-done.1, f32[2,64]{1,0:T(2,128)} %samples_ref.1, s32[3,4092]{1,0:T(4,128)} %chips_hbm.1, bf16[256,128]{1,0:T(8,128)(2,1)} %constant.18.clone.refs_0_, f32[2,128,128]{2,1,0:T(8,128)} %constant.19.clone.refs_1_, ...), custom_call_target="tpu_custom_call" | custom-call | tf_op jit(solution)/shard_map/compute/pallas_call | solution.py:412
  33.1 0.0 copy-start
  33.1 0.6 %copy-done = s32[3]{0:T(128)S(1)} copy-done((s32[3]{0:T(128)S(1)}, s32[3]{0:T(128)}, u32[]{:S(2)}) %copy-start) | copy-done | bytes 36
  33.8 2.1 %finish.1 = f32[3,128,1024]{2,1,0:T(8,128)} custom-call(s32[3]{0:T(128)S(1)} %copy-done, f32[4,8,128,128]{3,2,1,0:T(8,128)S(1)} %get-tuple-element.7.power_ref, f32[3,8,128]{2,1,0:T(8,128)S(1)} %get-tuple-element.8.mean_ref), custom_call_target="tpu_custom_call" | custom-call | tf_op jit(solution)/shard_map/finish/pallas_call | solution.py:468
Async XLA Ops:
  0.0 0.7 %copy-start.1 = (s32[3]{0:T(128)S(1)}, s32[3]{0:T(128)}, u32[]{:S(2)}) copy-start(s32[3]{0:T(128)} %centers_ref.1) | copy-start | bytes 40
  33.1 0.7 %copy-start = (s32[3]{0:T(128)S(1)}, s32[3]{0:T(128)}, u32[]{:S(2)}) copy-start(s32[3]{0:T(128)} %widths_ref.1) | copy-start | bytes 40

commit v6 on v5

--- a/solution.py
+++ b/solution.py
@@ -184,7 +184,7 @@
     )
 
 
-def mean_part(signal, window, code, mean_ref):
+def mean_part(signal, window, code, widths, mean_ref):
     size = signal[0:128, :] * signal[0:128, :] + signal[128:256, :] * signal[128:256, :]
     high, low = split(size)
     under = lax.dot_general(
@@ -196,7 +196,9 @@
     for s in range(SATS):
         re, im = code[s, 0], code[s, 1]
         total = jnp.sum(under * (re * re + im * im), axis=(0, 1), keepdims=True)
-        mean_ref[s] = jnp.broadcast_to(total * (1.0 / (DOP * N)), (8, 128))
+        mean = jnp.broadcast_to(total * (1.0 / (DOP * N)), (8, 128))
+        width = jnp.full((8, 128), widths[s].astype(F32))
+        mean_ref[s] = jnp.where(lax.broadcasted_iota(jnp.int32, (8, 128), 0) == 0, mean, width)
 
 
 EIGHTH = math.sqrt(0.5)
@@ -268,7 +270,7 @@
             store(t, rows, (a * a + b * b) * (1.0 / N))
 
 
-def main_part(signal, left_high, left_low, even, odd, wide, narrow, power_ref, own, send):
+def main_part(signal, left_high, left_low, even, odd, wide, narrow, power_ref, own, send, meanwhile):
     def both(lam, fill, drain):
         for kap in range(8):
             products(lam, signal, left_high, left_low, fill, kap)
@@ -314,23 +316,24 @@
         lax.fori_loop(first, last, one, 0, unroll=2)
 
     finish_wide(0, 8)
-    finish_narrow(0, 4)
+    finish_narrow(0, 2)
     copies = [send(0)]
     finish_wide(8, 16)
-    finish_narrow(4, 8)
+    finish_narrow(2, 4)
     copies.append(send(1))
-    finish_narrow(8, 16)
+    meanwhile()
+    finish_narrow(4, 16)
     for copy in copies:
         copy.wait()
 
 
-def compute_kernel(centers_ref, samples_ref, chips_hbm, *refs):
+def compute_kernel(centers_hbm, widths_hbm, samples_ref, chips_hbm, *refs):
     count = len(NAMES)
     hbm = dict(zip(NAMES, refs[:count]))
     power_ref, mean_ref = refs[count : count + 2]
     refs = refs[count + 2 :]
     table = dict(zip(NAMES, refs[:count]))
-    (gathered, chips, chip_rows, spectrum, code, left_high, left_low, signal, even, odd, wide, narrow,
+    (centers, widths, gathered, chips, chip_rows, spectrum, code, left_high, left_low, signal, even, odd, wide, narrow,
      own_sem, table_sem, send_sem, recv_sem) = refs[count:]
     sat = lax.axis_index("sat")
     dop = lax.axis_index("dop")
@@ -347,6 +350,10 @@
     own.start()
     loads = {"chips": pltpu.make_async_copy(chips_hbm, chips, table_sem.at[count])}
     loads["chips"].start()
+    loads["centers"] = pltpu.make_async_copy(centers_hbm, centers, table_sem.at[count + 1])
+    loads["centers"].start()
+    loads["widths"] = pltpu.make_async_copy(widths_hbm, widths, table_sem.at[count + 2])
+    loads["widths"].start()
     for i, name in enumerate(NAMES):
         loads[name] = pltpu.make_async_copy(hbm[name], table[name], table_sem.at[i])
         loads[name].start()
@@ -367,15 +374,15 @@
             copies[-1].start()
         return copies
 
-    for name in ("chips", "code_first", "code_twiddle", "right"):
+    for name in ("chips", "centers", "code_first", "code_twiddle", "right"):
         loads[name].wait()
-    code_part(centers_ref, chips, dop, table["code_first"], table["code_twiddle"], table["right"], chip_rows, spectrum, code)
+    code_part(centers, chips, dop, table["code_first"], table["code_twiddle"], table["right"], chip_rows, spectrum, code)
     own.wait()
     pl.semaphore_wait(barrier, 22)
     copies = exchange(0, 1, me, peers[:7], gathered.at[pl.ds(me, 1)])
     wide[...] = jnp.zeros_like(wide)
     narrow[...] = jnp.zeros_like(narrow)
-    for name in ("inverse", "step", "left", "signal_first", "signal_twiddle", "window"):
+    for name in ("widths", "inverse", "step", "left", "signal_first", "signal_twiddle", "window"):
         loads[name].wait()
     table_part(code, own_sat, table["inverse"], table["step"], left_high, left_low, 0, 3)
     for copy in copies:
@@ -386,7 +393,6 @@
         copy.wait()
     rows = jnp.concatenate([gathered[:, 0, :], gathered[:, 1, :]], 1)
     signal[...] = signal_part(rows, table["left"], table["signal_first"], table["signal_twiddle"])
-    mean_part(signal, table["window"], code, mean_ref)
 
     def send(half):
         rows = pl.ds(half * 64, 64)
@@ -401,24 +407,27 @@
         copy.start()
         return copy
 
-    main_part(signal, left_high, left_low, even, odd, wide, narrow, power_ref, own_sat, send)
+    main_part(signal, left_high, left_low, even, odd, wide, narrow, power_ref, own_sat, send,
+              lambda: mean_part(signal, table["window"], code, widths, mean_ref))
 
 
 def vmem():
     return pl.BlockSpec(memory_space=pltpu.VMEM)
 
 
-def computed(samples, chips, centers, tables):
+def computed(centers, widths, samples, chips, tables):
     return pl.pallas_call(
         compute_kernel,
         out_shape=[
             jax.ShapeDtypeStruct((SATS + 1, THI, 128, DOP), F32),
             jax.ShapeDtypeStruct((SATS, 8, 128), F32),
         ],
-        in_specs=[pl.BlockSpec(memory_space=pltpu.SMEM)] + [pl.BlockSpec(memory_space=pltpu.HBM)] * (2 + len(tables)),
+        in_specs=[pl.BlockSpec(memory_space=pltpu.HBM)] * (4 + len(tables)),
         out_specs=[vmem(), vmem()],
         scratch_shapes=[pltpu.VMEM(t.shape, t.dtype) for t in tables]
         + [
+            pltpu.SMEM((SATS,), jnp.int32),
+            pltpu.SMEM((SATS,), jnp.int32),
             pltpu.VMEM((128, 2, 64), F32),
             pltpu.VMEM((SATS, CHIPS), jnp.int32),
             pltpu.VMEM((96, 128), F32),
@@ -432,22 +441,22 @@
             pltpu.VMEM((2 * THI, 128, 256), F32),
             pltpu.VMEM((THI, 128, 256), F32),
             pltpu.SemaphoreType.DMA,
-            pltpu.SemaphoreType.DMA((len(tables) + 1,)),
+            pltpu.SemaphoreType.DMA((len(tables) + 3,)),
             pltpu.SemaphoreType.DMA((24,)),
             pltpu.SemaphoreType.DMA((24,)),
         ],
         compiler_params=pltpu.CompilerParams(vmem_limit_bytes=40 << 20, collective_id=0, has_side_effects=True),
         name="compute",
-    )(centers, samples, chips, *tables)
-
-
-def finish_kernel(widths_ref, power_ref, mean_ref, out_ref, ratios, sem):
+    )(centers, widths, samples, chips, *tables)
+
+
+def finish_kernel(power_ref, mean_ref, out_ref, ratios, sem):
     r = lax.broadcasted_iota(jnp.int32, (DOP, DOP), 0)
     q = lax.broadcasted_iota(jnp.int32, (DOP, DOP), 1)
     gap = jnp.abs(r - q)
     copies = []
     for s in range(SATS):
-        band = ((gap >= 2) & (gap <= 1 + widths_ref[s])).astype(F32)
+        band = ((gap >= 2) & (gap.astype(F32) <= 1.0 + mean_ref[s, 1:2, :])).astype(F32)
         scale = 1.0 / jnp.sum(band, axis=0, keepdims=True)
         band = band.astype(BF16)
         band = jnp.concatenate([band, band], 0)
@@ -464,24 +473,24 @@
         copy.wait()
 
 
-def finished(power, mean, widths):
+def finished(power, mean):
     return pl.pallas_call(
         finish_kernel,
         out_shape=jax.ShapeDtypeStruct((SATS, DOP, THI * 128), F32),
-        in_specs=[pl.BlockSpec(memory_space=pltpu.SMEM), vmem(), vmem()],
+        in_specs=[vmem(), vmem()],
         out_specs=pl.BlockSpec(memory_space=pl.ANY),
         scratch_shapes=[pltpu.VMEM((SATS, DOP, THI * 128), F32), pltpu.SemaphoreType.DMA((SATS,))],
         compiler_params=pltpu.CompilerParams(vmem_limit_bytes=16 << 20),
         name="finish",
-    )(widths, power, mean)
+    )(power, mean)
 
 
 def on_device(samples, code_chips, centers, widths):
     tables = build_tables()
-    places = [samples, code_chips] + [jnp.asarray(tables[n]) for n in NAMES]
+    places = [centers, widths, samples, code_chips] + [jnp.asarray(tables[n]) for n in NAMES]
     places = [pltpu.with_memory_space_constraint(a, pltpu.HBM) for a in places]
-    power, mean = computed(places[0], places[1], centers, places[2:])
-    return finished(power, mean, widths)
+    power, mean = computed(*places[:4], places[4:])
+    return finished(power, mean)
 
 
 def solution(mesh):

time: 36 us -> 33.3 us (0.925)
  local copies, waits for them, and re-layouts: 1.31 us -> 0 us
  Pallas kernels: 34.5 us -> 33.2 us
    unnamed x4 -> x0, local copies, waits for them, and re-layouts: 1.31 us -> none
    pallas_call x1, Pallas kernels: 32.4 us -> 31.6 us  [computed(): pl.pallas_call(compute_kernel, out_shape=[jax.ShapeDtypeStruct((SATS + 1,...]
    pallas_call x1, Pallas kernels: 2.12 us -> 1.56 us  [finished(): pl.pallas_call(finish_kernel, out_shape=jax.ShapeDtypeStruct((SATS, DOP,...]
where the time goes in v6:
time: 33.3 us; the launch traced here: 33.2 us
  Pallas kernels  33.2 us (100%)
    pallas_call x1, Pallas kernels, computed(): pl.pallas_call(compute_kernel, out_shape=[jax.ShapeDtypeStruct((SATS + 1,...  31.6 us
    pallas_call x1, Pallas kernels, finished(): pl.pallas_call(finish_kernel, out_shape=jax.ShapeDtypeStruct((SATS, DOP,...  1.56 us

profile of v6, /device:TPU:1, one launch (start us, length us, event | category | flops | bytes accessed | tf_op | source)
XLA Modules:
  0.0 33.2 jit_solution(13877464530688262874)
XLA Ops:
  0.0 31.6 %compute.1 = (f32[4,8,128,128]{3,2,1,0:T(8,128)S(1)}, f32[3,8,128]{2,1,0:T(8,128)S(1)}) custom-call(s32[3]{0:T(128)} %centers_hbm.1, s32[3]{0:T(128)} %widths_hbm.1, f32[2,64]{1,0:T(2,128)} %samples_ref.1, s32[3,4092]{1,0:T(4,128)} %chips_hbm.1, bf16[256,128]{1,0:T(8,128)(2,1)} %constant.18.clone.refs_0_, f32[2,128,128]{2,1,0:T(8,128)} %constant.19.clone.refs_1_, ...), custom_call_target="tpu_custom_call" | custom-call | tf_op jit(solution)/shard_map/compute/pallas_call | solution.py:419
  31.7 1.6 %finish.1 = f32[3,128,1024]{2,1,0:T(8,128)} custom-call(f32[4,8,128,128]{3,2,1,0:T(8,128)S(1)} %get-tuple-element.7.power_ref, f32[3,8,128]{2,1,0:T(8,128)S(1)} %get-tuple-element.8.mean_ref), custom_call_target="tpu_custom_call" | custom-call | tf_op jit(solution)/shard_map/finish/pallas_call | solution.py:477

commit v7 on v6

--- a/solution.py
+++ b/solution.py
@@ -230,14 +230,13 @@
     return [add(e[i], w[i]) for i in range(4)] + [sub(e[i], w[i]) for i in range(4)]
 
 
-def products(lam, signal, left_high, left_low, stage, kap):
-    k = lam + 8 * kap
+def windows(k, signal):
     lane = lax.broadcasted_iota(jnp.int32, (256, 128), 1)
     shift = 128 - 2 * k
     window = jnp.where(
         lane < shift,
-        pltpu.roll(signal[0:256, 0:128], shift, 1),
-        pltpu.roll(signal[0:256, 128:256], shift, 1),
+        pltpu.roll(signal[:, 0:128], shift, 1),
+        pltpu.roll(signal[:, 128:256], shift, 1),
     )
     high, low = split(window)
 
@@ -245,7 +244,11 @@
         re, im = part[:128], part[128:]
         return jnp.concatenate([jnp.concatenate([re, im], 1), jnp.concatenate([-im, re], 1)], 0)
 
-    high, low = embedded(high), embedded(low)
+    return embedded(high), embedded(low)
+
+
+def products(k, kap, factors, left_high, left_low, stage):
+    high, low = factors
     m_high, m_low = left_high[k], left_low[k]
     stage[kap] = dot(jnp.concatenate([m_high, m_low, m_high], 1), jnp.concatenate([high, high, low], 0))
 
@@ -261,7 +264,10 @@
         c, d = total[t, rows, 0:128], total[t, rows, 128:256]
         if t:
             cos, sin = math.cos(math.pi * t / 32), math.sin(math.pi * t / 32)
-            c, d = c * cos - d * sin, c * sin + d * cos
+            if t == 8:
+                c, d = (c - d) * EIGHTH, (c + d) * EIGHTH
+            else:
+                c, d = c * cos - d * sin, c * sin + d * cos
         a, b = a + c, b + d
         if store is None:
             total[t, rows, 0:128] = a
@@ -270,16 +276,20 @@
             store(t, rows, (a * a + b * b) * (1.0 / N))
 
 
-def main_part(signal, left_high, left_low, even, odd, wide, narrow, power_ref, own, send, meanwhile):
+def main_part(signal, left_high, left_low, even, odd, wide, narrow, power_ref, own, send, meanwhile, ready):
     def both(lam, fill, drain):
         for kap in range(8):
-            products(lam, signal, left_high, left_low, fill, kap)
+            k = lam + 8 * kap
+            factors = windows(k, signal) if kap else (ready[0], ready[1])
+            products(k, kap, factors, left_high, left_low, fill)
             for g in range(2):
                 combine(drain, wide, 0, kap * 16 + g * 8)
                 combine(drain, narrow, 1, kap * 16 + g * 8)
+        ready[0], ready[1] = windows(jnp.maximum(lam - 1, 0), signal)
 
     for kap in range(8):
-        products(7, signal, left_high, left_low, odd, kap)
+        products(7 + 8 * kap, kap, windows(7 + 8 * kap, signal), left_high, left_low, odd)
+    ready[0], ready[1] = windows(6, signal)
 
     def step(i, _):
         @pl.when(i % 2 == 0)
@@ -333,7 +343,7 @@
     power_ref, mean_ref = refs[count : count + 2]
     refs = refs[count + 2 :]
     table = dict(zip(NAMES, refs[:count]))
-    (centers, widths, gathered, chips, chip_rows, spectrum, code, left_high, left_low, signal, even, odd, wide, narrow,
+    (centers, widths, gathered, chips, chip_rows, spectrum, code, left_high, left_low, signal, even, odd, wide, narrow, ready,
      own_sem, table_sem, send_sem, recv_sem) = refs[count:]
     sat = lax.axis_index("sat")
     dop = lax.axis_index("dop")
@@ -408,7 +418,7 @@
         return copy
 
     main_part(signal, left_high, left_low, even, odd, wide, narrow, power_ref, own_sat, send,
-              lambda: mean_part(signal, table["window"], code, widths, mean_ref))
+              lambda: mean_part(signal, table["window"], code, widths, mean_ref), ready)
 
 
 def vmem():
@@ -440,6 +450,7 @@
             pltpu.VMEM((8, 256, 256), F32),
             pltpu.VMEM((2 * THI, 128, 256), F32),
             pltpu.VMEM((THI, 128, 256), F32),
+            pltpu.VMEM((2, 256, 256), BF16),
             pltpu.SemaphoreType.DMA,
             pltpu.SemaphoreType.DMA((len(tables) + 3,)),
             pltpu.SemaphoreType.DMA((24,)),

time: 33.3 us -> 31.9 us (0.958)
  Pallas kernels: 33.2 us -> 31.8 us
    pallas_call x1, Pallas kernels: 31.6 us -> 30.3 us  [computed(): pl.pallas_call(compute_kernel, out_shape=[jax.ShapeDtypeStruct((SATS + 1,...]
where the time goes in v7:
time: 31.9 us; the launch traced here: 31.8 us
  Pallas kernels  31.8 us (100%)
    pallas_call x1, Pallas kernels, computed(): pl.pallas_call(compute_kernel, out_shape=[jax.ShapeDtypeStruct((SATS + 1,...  30.3 us
    pallas_call x1, Pallas kernels, finished(): pl.pallas_call(finish_kernel, out_shape=jax.ShapeDtypeStruct((SATS, DOP,...  1.56 us

profile of v7, /device:TPU:1, one launch (start us, length us, event | category | flops | bytes accessed | tf_op | source)
XLA Modules:
  0.0 31.8 jit_solution(2722896432292818239)
XLA Ops:
  0.0 30.3 %compute.1 = (f32[4,8,128,128]{3,2,1,0:T(8,128)S(1)}, f32[3,8,128]{2,1,0:T(8,128)S(1)}) custom-call(s32[3]{0:T(128)} %centers_hbm.1, s32[3]{0:T(128)} %widths_hbm.1, f32[2,64]{1,0:T(2,128)} %samples_ref.1, s32[3,4092]{1,0:T(4,128)} %chips_hbm.1, bf16[256,128]{1,0:T(8,128)(2,1)} %constant.18.clone.refs_0_, f32[2,128,128]{2,1,0:T(8,128)} %constant.19.clone.refs_1_, ...), custom_call_target="tpu_custom_call" | custom-call | tf_op jit(solution)/shard_map/compute/pallas_call | solution.py:429
  30.3 1.6 %finish.1 = f32[3,128,1024]{2,1,0:T(8,128)} custom-call(f32[4,8,128,128]{3,2,1,0:T(8,128)S(1)} %get-tuple-element.7.power_ref, f32[3,8,128]{2,1,0:T(8,128)S(1)} %get-tuple-element.8.mean_ref), custom_call_target="tpu_custom_call" | custom-call | tf_op jit(solution)/shard_map/finish/pallas_call | solution.py:488

commit v8 on v7

--- a/solution.py
+++ b/solution.py
@@ -233,18 +233,17 @@
 def windows(k, signal):
     lane = lax.broadcasted_iota(jnp.int32, (256, 128), 1)
     shift = 128 - 2 * k
-    window = jnp.where(
-        lane < shift,
-        pltpu.roll(signal[:, 0:128], shift, 1),
-        pltpu.roll(signal[:, 128:256], shift, 1),
-    )
-    high, low = split(window)
-
-    def embedded(part):
+
+    def embedded(i):
+        part = jnp.where(
+            lane < shift,
+            pltpu.roll(signal[i, :, 0:128], shift, 1),
+            pltpu.roll(signal[i, :, 128:256], shift, 1),
+        )
         re, im = part[:128], part[128:]
         return jnp.concatenate([jnp.concatenate([re, im], 1), jnp.concatenate([-im, re], 1)], 0)
 
-    return embedded(high), embedded(low)
+    return embedded(0), embedded(1)
 
 
 def products(k, kap, factors, left_high, left_low, stage):
@@ -253,7 +252,7 @@
     stage[kap] = dot(jnp.concatenate([m_high, m_low, m_high], 1), jnp.concatenate([high, high, low], 0))
 
 
-def combine(stage, total, slot, row, store=None):
+def combine(stage, total, slot, row, store=None, first=False):
     rows = pl.ds(row, 8)
     from_rows = pl.ds(slot * 128 + row, 8)
     re = [stage[kap, from_rows, 0:128] for kap in range(8)]
@@ -261,14 +260,14 @@
     out = dft8(re, im)
     for t in range(total.shape[0]):
         a, b = out[t % 8]
-        c, d = total[t, rows, 0:128], total[t, rows, 128:256]
-        if t:
+        if not first:
+            c, d = total[t, rows, 0:128], total[t, rows, 128:256]
             cos, sin = math.cos(math.pi * t / 32), math.sin(math.pi * t / 32)
             if t == 8:
                 c, d = (c - d) * EIGHTH, (c + d) * EIGHTH
-            else:
+            elif t:
                 c, d = c * cos - d * sin, c * sin + d * cos
-        a, b = a + c, b + d
+            a, b = a + c, b + d
         if store is None:
             total[t, rows, 0:128] = a
             total[t, rows, 128:256] = b
@@ -276,17 +275,19 @@
             store(t, rows, (a * a + b * b) * (1.0 / N))
 
 
-def main_part(signal, left_high, left_low, even, odd, wide, narrow, power_ref, own, send, meanwhile, ready):
-    def both(lam, fill, drain):
+def main_part(signal_full, left_high, left_low, even, odd, wide, narrow, power_ref, own, send, meanwhile, ready, pieces):
+    def both(lam, fill, drain, first=False):
         for kap in range(8):
             k = lam + 8 * kap
             factors = windows(k, signal) if kap else (ready[0], ready[1])
             products(k, kap, factors, left_high, left_low, fill)
             for g in range(2):
-                combine(drain, wide, 0, kap * 16 + g * 8)
-                combine(drain, narrow, 1, kap * 16 + g * 8)
+                combine(drain, wide, 0, kap * 16 + g * 8, first=first)
+                combine(drain, narrow, 1, kap * 16 + g * 8, first=first)
         ready[0], ready[1] = windows(jnp.maximum(lam - 1, 0), signal)
 
+    signal = pieces
+    signal[0], signal[1] = split(signal_full[...])
     for kap in range(8):
         products(7 + 8 * kap, kap, windows(7 + 8 * kap, signal), left_high, left_low, odd)
     ready[0], ready[1] = windows(6, signal)
@@ -302,7 +303,8 @@
 
         return 0
 
-    lax.fori_loop(0, 7, step, 0)
+    both(6, even, odd, first=True)
+    lax.fori_loop(1, 7, step, 0)
     places = [jnp.where(own == half, own, 3) for half in range(2)]
 
     def keep_wide(t, rows, value):
@@ -343,7 +345,7 @@
     power_ref, mean_ref = refs[count : count + 2]
     refs = refs[count + 2 :]
     table = dict(zip(NAMES, refs[:count]))
-    (centers, widths, gathered, chips, chip_rows, spectrum, code, left_high, left_low, signal, even, odd, wide, narrow, ready,
+    (centers, widths, gathered, chips, chip_rows, spectrum, code, left_high, left_low, signal, even, odd, wide, narrow, ready, pieces,
      own_sem, table_sem, send_sem, recv_sem) = refs[count:]
     sat = lax.axis_index("sat")
     dop = lax.axis_index("dop")
@@ -390,8 +392,6 @@
     own.wait()
     pl.semaphore_wait(barrier, 22)
     copies = exchange(0, 1, me, peers[:7], gathered.at[pl.ds(me, 1)])
-    wide[...] = jnp.zeros_like(wide)
-    narrow[...] = jnp.zeros_like(narrow)
     for name in ("widths", "inverse", "step", "left", "signal_first", "signal_twiddle", "window"):
         loads[name].wait()
     table_part(code, own_sat, table["inverse"], table["step"], left_high, left_low, 0, 3)
@@ -418,7 +418,7 @@
         return copy
 
     main_part(signal, left_high, left_low, even, odd, wide, narrow, power_ref, own_sat, send,
-              lambda: mean_part(signal, table["window"], code, widths, mean_ref), ready)
+              lambda: mean_part(signal, table["window"], code, widths, mean_ref), ready, pieces)
 
 
 def vmem():
@@ -451,6 +451,7 @@
             pltpu.VMEM((2 * THI, 128, 256), F32),
             pltpu.VMEM((THI, 128, 256), F32),
             pltpu.VMEM((2, 256, 256), BF16),
+            pltpu.VMEM((2, 256, 256), BF16),
             pltpu.SemaphoreType.DMA,
             pltpu.SemaphoreType.DMA((len(tables) + 3,)),
             pltpu.SemaphoreType.DMA((24,)),

time: 31.9 us -> 31.6 us (level)
    pallas_call x1, Pallas kernels: 30.3 us -> 29.9 us  [computed(): pl.pallas_call(compute_kernel, out_shape=[jax.ShapeDtypeStruct((SATS + 1,...]
where the time goes in v8:
time: 31.6 us; the launch traced here: 31.5 us
  Pallas kernels  31.5 us (100%)
    pallas_call x1, Pallas kernels, computed(): pl.pallas_call(compute_kernel, out_shape=[jax.ShapeDtypeStruct((SATS + 1,...  29.9 us
    pallas_call x1, Pallas kernels, finished(): pl.pallas_call(finish_kernel, out_shape=jax.ShapeDtypeStruct((SATS, DOP,...  1.56 us

profile of v8, /device:TPU:1, one launch (start us, length us, event | category | flops | bytes accessed | tf_op | source)
XLA Modules:
  0.0 31.5 jit_solution(11032592261872074926)
XLA Ops:
  0.0 29.9 %compute.1 = (f32[4,8,128,128]{3,2,1,0:T(8,128)S(1)}, f32[3,8,128]{2,1,0:T(8,128)S(1)}) custom-call(s32[3]{0:T(128)} %centers_hbm.1, s32[3]{0:T(128)} %widths_hbm.1, f32[2,64]{1,0:T(2,128)} %samples_ref.1, s32[3,4092]{1,0:T(4,128)} %chips_hbm.1, bf16[256,128]{1,0:T(8,128)(2,1)} %constant.18.clone.refs_0_, f32[2,128,128]{2,1,0:T(8,128)} %constant.19.clone.refs_1_, ...), custom_call_target="tpu_custom_call" | custom-call | tf_op jit(solution)/shard_map/compute/pallas_call | solution.py:429
  29.9 1.6 %finish.1 = f32[3,128,1024]{2,1,0:T(8,128)} custom-call(f32[4,8,128,128]{3,2,1,0:T(8,128)S(1)} %get-tuple-element.7.power_ref, f32[3,8,128]{2,1,0:T(8,128)S(1)} %get-tuple-element.8.mean_ref), custom_call_target="tpu_custom_call" | custom-call | tf_op jit(solution)/shard_map/finish/pallas_call | solution.py:489
